TPU v7x, 32 devices: a whole 2x2x4 slice. The times are simulated.
32 devices in a mesh: dp: 8 (over y, x, core), tensor: 4 (over z).
Axes of the slice: x: 2, y: 2, z: 4, core: 2. Of those that a mesh axis runs over, the one named last changes fastest.
Arguments:
- tokens: bfloat16 [16, 2048, 768], P('dp', 'tensor'), may hold values from -6 to 6
- segments: int32 [16, 2048], P('dp'), may hold values from 0 to 3, never falling along the last dimension, each value on 1 to 800 neighbouring positions
- pairing: int32 [12, 4], P('tensor'), may hold values from 0 to 3, each once within a row
- qkv_weight: bfloat16 [768, 12, 192], P('dp', 'tensor'), may hold values from -0.3125 to 0.3125
- qv_bias: bfloat16 [12, 128], P('tensor'), may hold values from -3 to 3
- out_weight: bfloat16 [12, 64, 768], P('tensor', None, 'dp'), may hold values from -0.875 to 0.875
- out_bias: bfloat16 [768], replicated, may hold values from -3 to 3
- first_gain: bfloat16 [768], replicated, may hold values from 0.5 to 1.5
- first_shift: bfloat16 [768], replicated, may hold values from -2 to 2
- up_weight: bfloat16 [768, 3072], P('dp', 'tensor'), may hold values from -0.21875 to 0.21875
- up_bias: bfloat16 [3072], P('tensor'), may hold values from -3 to 3
- down_weight: bfloat16 [3072, 768], P('tensor', 'dp'), may hold values from -0.109375 to 0.109375
- down_bias: bfloat16 [768], replicated, may hold values from -3 to 3
- second_gain: bfloat16 [768], replicated, may hold values from 0.5 to 1.5
- second_shift: bfloat16 [768], replicated, may hold values from -2 to 2
- cotangent: bfloat16 [16, 2048, 768], P('dp', 'tensor'), may hold values from -6 to 6
Outputs:
- layer_out: bfloat16 [16, 2048, 768], P('dp', 'tensor')
- input_grad: bfloat16 [16, 2048, 768], P('dp', 'tensor')
- qkv_weight_grad: float32 [768, 12, 192], P('dp', 'tensor')
- qv_bias_grad: float32 [12, 128], P('tensor')
- out_weight_grad: float32 [12, 64, 768], P('tensor', None, 'dp')
- out_bias_grad: float32 [768], replicated
- first_gain_grad: float32 [768], replicated
- first_shift_grad: float32 [768], replicated
- up_weight_grad: float32 [768, 3072], P('dp', 'tensor')
- up_bias_grad: float32 [3072], P('tensor')
- down_weight_grad: float32 [3072, 768], P('tensor', 'dp')
- down_bias_grad: float32 [768], replicated
- second_gain_grad: float32 [768], replicated
- second_shift_grad: float32 [768], replicated
Inputs may be any that keep to these rules, and one draw needn't show every extreme that they name: `segments`: along each sequence the numbers never fall; each number covers at most 800 positions of its sequence, and one covers exactly 800. `pairing`: each row holds every number from 0 to 3 once.
All inputs are finite; a program needn't handle non-finite values.
Results may differ from a plain program's by a relative error of at most 0.013.
Values may be sent and summed in bfloat16 or wider, within the bound.
No kernel may reach another device: no remote copies, remote signals or barrier semaphores. Data moves between devices by JAX's collectives and lax.ppermute only.
A program may use at most 192 MiB of HBM per device.

v0:
```python
import functools

import jax
import jax.numpy as jnp
from jax import lax
from jax.experimental import pallas as pl
from jax.experimental.pallas import tpu as pltpu
from jax.sharding import PartitionSpec as P

EPS = 1e-06
NEG = -1e30
BOTH = ("dp", "tensor")
F32 = jnp.float32
BF16 = jnp.bfloat16
ANY = pl.BlockSpec(memory_space=pl.ANY)
LIMIT = 58 << 20


def mm(left, right):
    return lax.dot_general(left, right, (((1,), (0,)), ((), ())), preferred_element_type=F32)


def mm_rt(left, right):
    return lax.dot_general(left, right, (((1,), (1,)), ((), ())), preferred_element_type=F32)


def mm_lt(left, right):
    return lax.dot_general(left, right, (((0,), (0,)), ((), ())), preferred_element_type=F32)


def head_lanes(shape, head, dim, head_size):
    place = lax.broadcasted_iota(jnp.int32, shape, dim)
    return (place < head_size) if head == 0 else (place >= head_size)


def fetches(pieces, offsets, target, dim, sems, first):
    copies = []
    for k, (piece, offset) in enumerate(zip(pieces, offsets)):
        count = piece.shape[dim]
        where = pl.ds(offset if isinstance(offset, int) else pl.multiple_of(offset, count), count)
        index = (slice(None),) * dim + (where,)
        copies.append(pltpu.make_async_copy(piece, target.at[index], sems.at[first + k]))
    return copies


def piece_rows(place, step, rows, count):
    if count == 1:
        return [0]
    return [(place ^ (k * step)) * rows for k in range(count)]


def attend_kernel(pair_ref, place_ref, *refs, rows, hs, blocks, n_w):
    x_refs, refs = refs[:blocks], refs[blocks:]
    w_refs, refs = refs[:n_w], refs[n_w:]
    bias_ref, segq_ref, segk_ref, q_out, k_out, v_out, o_ref, lse_ref, x_all, w_all, sems = refs
    group, block = pl.program_id(0), pl.program_id(1)
    lanes2 = 2 * hs

    @pl.when((group == 0) & (block == 0))
    def _():
        chip = place_ref[0] // 2
        copies = fetches(
            w_refs, piece_rows(chip, 1, w_refs[0].shape[1], n_w), w_all, 1, sems, 0
        ) + fetches(x_refs, [rows * k for k in range(blocks)], x_all, 0, sems, n_w)
        for copy in copies:
            copy.start()
        for copy in copies:
            copy.wait()

    @pl.when(block == 0)
    def _():
        weight = w_all[group]
        for k in range(blocks):
            part = pl.ds(k * rows, rows)
            out = (mm(x_all[part, :], weight) + bias_ref[0]).astype(BF16)
            q_out[part, :] = out[:, :lanes2] * (hs**-0.5)
            k_out[part, :] = out[:, lanes2 : 2 * lanes2]
            v_out[part, :] = out[:, 2 * lanes2 :]

    own = pl.ds(pl.multiple_of(block * rows, rows), rows)
    q2 = q_out[own, :]
    own_raw = (q2.astype(F32) * k_out[own, :].astype(F32)).T
    own_values = v_out[own, :].astype(F32).T
    segq = segq_ref[...]
    total = jnp.zeros((2 * hs, rows), F32)
    for head in range(2):
        target = pair_ref[2 * group + head, block]
        there = pl.ds(pl.multiple_of(target * rows, rows), rows)
        keys, values = k_out[there, :], v_out[there, :]
        lanes = head_lanes(q2.shape, head, 1, hs)
        scores = mm_rt(keys, jnp.where(lanes, q2, jnp.zeros_like(q2)))
        scores = jnp.where(segk_ref[there, :] == segq, scores, NEG)
        raw = jnp.sum(own_raw[head * hs : (head + 1) * hs], axis=0, keepdims=True)
        raw = jnp.where(target != block, raw, NEG)
        peak = jnp.maximum(jnp.max(scores, axis=0, keepdims=True), raw)
        expo = jnp.exp(scores - peak)
        own_expo = jnp.exp(raw - peak)
        denom = jnp.sum(expo, axis=0, keepdims=True) + own_expo
        masked_values = jnp.where(lanes, values, jnp.zeros_like(values))
        part = mm_lt(masked_values, expo.astype(BF16))
        low = own_expo.astype(BF16).astype(F32)
        mine = head_lanes(part.shape, head, 0, hs)
        part = part + jnp.where(mine, own_values * low, 0.0)
        total = total + part * (1.0 / denom)
        lse_ref[0, head : head + 1, :] = peak + jnp.log(denom)
    o_ref[...] = total.T.astype(BF16)


def attend(pairs, place, x_parts, w_pieces, bias, segq, segk, hs):
    heads, blocks = pairs.shape
    rows, width = x_parts[0].shape
    seq, groups, lanes = rows * blocks, heads // 2, 2 * hs
    kept = jax.ShapeDtypeStruct((seq, groups * lanes), BF16)
    flops = 2 * seq * width * 3 * groups * lanes + 4 * heads * seq * rows * 2 * lanes
    return pl.pallas_call(
        functools.partial(attend_kernel, rows=rows, hs=hs, blocks=blocks, n_w=len(w_pieces)),
        grid_spec=pltpu.PrefetchScalarGridSpec(
            num_scalar_prefetch=2,
            grid=(groups, blocks),
            in_specs=[ANY] * (blocks + len(w_pieces))
            + [
                pl.BlockSpec((1, 1, 3 * lanes), lambda g, i, p, q: (g, 0, 0)),
                pl.BlockSpec((1, rows), lambda g, i, p, q: (0, i)),
                pl.BlockSpec((seq, 1), lambda g, i, p, q: (0, 0)),
            ],
            out_specs=[pl.BlockSpec((seq, lanes), lambda g, i, p, q: (0, g))] * 3
            + [
                pl.BlockSpec((rows, lanes), lambda g, i, p, q: (i, g)),
                pl.BlockSpec((1, 8, rows), lambda g, i, p, q: (g, 0, i)),
            ],
            scratch_shapes=[
                pltpu.VMEM((seq, width), BF16),
                pltpu.VMEM((groups, width, 3 * lanes), BF16),
                pltpu.SemaphoreType.DMA((blocks + len(w_pieces),)),
            ],
        ),
        out_shape=[kept, kept, kept, kept, jax.ShapeDtypeStruct((groups, 8, seq), F32)],
        compiler_params=pltpu.CompilerParams(vmem_limit_bytes=LIMIT),
        cost_estimate=pl.CostEstimate(flops=flops, bytes_accessed=20 << 20, transcendentals=0),
        name="attend",
    )(pairs, place, *x_parts, *w_pieces, bias, segq, segk)


def attend_back_kernel(pair_ref, place_ref, *refs, rows, hs, blocks, groups, n_w):
    x_refs, refs = refs[:blocks], refs[blocks:]
    w_refs, refs = refs[:n_w], refs[n_w:]
    (
        q_ref, k_ref, v_ref, do_ref, segq_ref, segk_ref, lse_ref,
        dw_ref, in_mine, in_other, sums_ref,
        x_all, x_t, w_all, in_acc, dq_all, dk_acc, dv_acc, sems,
    ) = refs
    group, block = pl.program_id(0), pl.program_id(1)

    @pl.when((group == 0) & (block == 0))
    def _():
        chip = place_ref[0] // 2
        copies = fetches(
            w_refs, piece_rows(chip, 1, w_refs[0].shape[1], n_w), w_all, 1, sems, 0
        ) + fetches(x_refs, [rows * k for k in range(blocks)], x_all, 0, sems, n_w)
        for copy in copies:
            copy.start()
        for copy in copies:
            copy.wait()
        for k in range(blocks):
            x_t[:, rows * k : rows * (k + 1)] = x_all[rows * k : rows * (k + 1), :].T
        in_acc[...] = jnp.zeros_like(in_acc)

    @pl.when(block == 0)
    def _():
        dk_acc[...] = jnp.zeros_like(dk_acc)
        dv_acc[...] = jnp.zeros_like(dv_acc)
        sums_ref[...] = jnp.zeros_like(sums_ref)

    own = pl.ds(pl.multiple_of(block * rows, rows), rows)
    q2, do2 = q_ref[...], do_ref[...]
    qt, dot = q2.astype(F32).T, do2.astype(F32).T
    own_keys, own_values = k_ref[own, :].astype(F32).T, v_ref[own, :].astype(F32).T
    own_raw, own_dp = qt * own_keys, dot * own_values
    segq = segq_ref[...]
    dq = jnp.zeros((2 * hs, rows), F32)
    own_ds, own_low = [], []
    for head in range(2):
        target = pair_ref[2 * group + head, block]
        there = pl.ds(pl.multiple_of(target * rows, rows), rows)
        keys, values = k_ref[there, :], v_ref[there, :]
        lanes = head_lanes(q2.shape, head, 1, hs)
        zero = jnp.zeros_like(q2)
        qm, dom = jnp.where(lanes, q2, zero), jnp.where(lanes, do2, zero)
        lse = lse_ref[0, head : head + 1, :]
        scores = mm_rt(keys, qm)
        probs = jnp.exp(jnp.where(segk_ref[there, :] == segq, scores - lse, NEG))
        raw = jnp.sum(own_raw[head * hs : (head + 1) * hs], axis=0, keepdims=True)
        self_prob = jnp.exp(jnp.where(target != block, raw - lse, NEG))
        self_dp = jnp.sum(own_dp[head * hs : (head + 1) * hs], axis=0, keepdims=True)
        dv_acc[there, :] += mm(probs.astype(BF16), dom)
        dprobs = mm_rt(values, dom)
        delta = jnp.sum(probs * dprobs, axis=0, keepdims=True) + self_prob * self_dp
        dscores = (probs * (dprobs - delta)).astype(BF16)
        dk_acc[there, :] += mm(dscores, qm)
        dq = dq + mm_lt(jnp.where(lanes, keys, jnp.zeros_like(keys)), dscores)
        own_ds.append((self_prob * (self_dp - delta)).astype(BF16).astype(F32))
        own_low.append(self_prob.astype(BF16).astype(F32))
    first = head_lanes(dq.shape, 0, 0, hs)
    ds_rows = jnp.where(first, own_ds[0], own_ds[1])
    low_rows = jnp.where(first, own_low[0], own_low[1])
    dq = ((dq + ds_rows * own_keys) * (hs**-0.5)).T
    dq_all[own, :] = dq.astype(BF16)
    sums_ref[0, 0:1, :] += jnp.sum(dq, axis=0, keepdims=True)
    dk_acc[own, :] += (ds_rows * qt).T
    dv_acc[own, :] += (low_rows * dot).T

    @pl.when(block == blocks - 1)
    def _():
        dv = dv_acc[...]
        sums_ref[0, 1:2, :] = jnp.sum(dv, axis=0, keepdims=True)
        packed = jnp.concatenate([dq_all[...], dk_acc[...].astype(BF16), dv.astype(BF16)], axis=1)
        dw_ref[0] = mm(x_t[...], packed)
        in_acc[...] += mm_rt(packed, w_all[group])

    @pl.when((block == blocks - 1) & (group == groups - 1))
    def _():
        half = blocks // 2 * rows
        in_mine[...] = in_acc[:half, :]
        in_other[...] = in_acc[half:, :].astype(BF16)


def attend_back(pairs, place, x_parts, w_pieces, q, k, v, grad_mixed, segq, segk, lse, hs):
    heads, blocks = pairs.shape
    rows, width = x_parts[0].shape
    seq, groups, lanes = rows * blocks, heads // 2, 2 * hs
    half = blocks // 2 * rows
    flops = 4 * seq * width * 3 * groups * lanes + 10 * heads * seq * rows * 2 * lanes
    return pl.pallas_call(
        functools.partial(
            attend_back_kernel, rows=rows, hs=hs, blocks=blocks, groups=groups, n_w=len(w_pieces)
        ),
        grid_spec=pltpu.PrefetchScalarGridSpec(
            num_scalar_prefetch=2,
            grid=(groups, blocks),
            in_specs=[ANY] * (blocks + len(w_pieces))
            + [
                pl.BlockSpec((rows, lanes), lambda g, i, p, q: (i, g)),
                pl.BlockSpec((seq, lanes), lambda g, i, p, q: (0, g)),
                pl.BlockSpec((seq, lanes), lambda g, i, p, q: (0, g)),
                pl.BlockSpec((rows, lanes), lambda g, i, p, q: (i, g)),
                pl.BlockSpec((1, rows), lambda g, i, p, q: (0, i)),
                pl.BlockSpec((seq, 1), lambda g, i, p, q: (0, 0)),
                pl.BlockSpec((1, 8, rows), lambda g, i, p, q: (g, 0, i)),
            ],
            out_specs=[
                pl.BlockSpec((1, width, 3 * lanes), lambda g, i, p, q: (g, 0, 0)),
                pl.BlockSpec((half, width), lambda g, i, p, q: (0, 0)),
                pl.BlockSpec((half, width), lambda g, i, p, q: (0, 0)),
                pl.BlockSpec((1, 8, lanes), lambda g, i, p, q: (g, 0, 0)),
            ],
            scratch_shapes=[
                pltpu.VMEM((seq, width), BF16),
                pltpu.VMEM((width, seq), BF16),
                pltpu.VMEM((groups, width, 3 * lanes), BF16),
                pltpu.VMEM((seq, width), F32),
                pltpu.VMEM((seq, lanes), BF16),
                pltpu.VMEM((seq, lanes), F32),
                pltpu.VMEM((seq, lanes), F32),
                pltpu.SemaphoreType.DMA((blocks + len(w_pieces),)),
            ],
        ),
        out_shape=[
            jax.ShapeDtypeStruct((groups, width, 3 * lanes), F32),
            jax.ShapeDtypeStruct((half, width), F32),
            jax.ShapeDtypeStruct((half, width), BF16),
            jax.ShapeDtypeStruct((groups, 8, lanes), F32),
        ],
        compiler_params=pltpu.CompilerParams(vmem_limit_bytes=LIMIT),
        cost_estimate=pl.CostEstimate(flops=flops, bytes_accessed=30 << 20, transcendentals=0),
        name="attend_back",
    )(pairs, place, *x_parts, *w_pieces, q, k, v, grad_mixed, segq, segk, lse)


def norm(values):
    centred = values - jnp.mean(values, axis=-1, keepdims=True)
    scale = lax.rsqrt(jnp.mean(centred * centred, axis=-1, keepdims=True) + EPS)
    return centred * scale, scale


def norm_back(grad, unit, scale, gain):
    q = grad * gain
    mean_q = jnp.mean(q, axis=-1, keepdims=True)
    mean_qn = jnp.mean(q * unit, axis=-1, keepdims=True)
    return scale * (q - mean_q - unit * mean_qn)


def gelu_parts(u):
    dense = jnp.exp(-0.5 * u * u) * 0.3989422804014327
    t = 1.0 / (1.0 + 0.2316419 * jnp.abs(u))
    poly = t * (
        0.319381530
        + t * (-0.356563782 + t * (1.781477937 + t * (-1.821255978 + t * 1.330274429)))
    )
    tail = dense * poly
    phi = jnp.where(u >= 0, 1.0 - tail, tail)
    return u * phi, phi + u * dense


def dense_kernel(place_ref, *refs, n_o, n_w, chunks):
    o_refs, refs = refs[:n_o], refs[n_o:]
    w_refs, refs = refs[:n_w], refs[n_w:]
    (
        x_ref, mine_ref, other_ref, cot_ref, vec_ref, upb_ref,
        layer_ref, gm_mine, gm_other, act_ref, mlow_ref, gb_ref, gul_ref, ga_ref, gone_ref, sums_ref, upsum_ref,
        wo, ww, slope, acc, sems,
    ) = refs
    step = pl.program_id(0)
    core = place_ref[0] % 2
    cols = mine_ref.shape[1]
    width = x_ref.shape[1]
    units = ww.shape[2] // 2

    @pl.when(step == 0)
    def _():
        o_copies = fetches(o_refs, piece_rows(place_ref[0], 1, o_refs[0].shape[0], n_o), wo, 0, sems, 0)
        w_copies = fetches(w_refs, piece_rows(place_ref[0], 1, w_refs[0].shape[1], n_w), ww, 1, sems, n_o)
        for copy in o_copies + w_copies:
            copy.start()
        for copy in o_copies + w_copies:
            copy.wait()
        sums_ref[...] = jnp.zeros_like(sums_ref)
        upsum_ref[...] = jnp.zeros_like(upsum_ref)

    mine_cols = pl.ds(pl.multiple_of(core * cols, cols), cols)
    other_cols = pl.ds(pl.multiple_of((1 - core) * cols, cols), cols)
    attn = mm_rt(mine_ref[...], wo[:, mine_cols]) + mm_rt(other_ref[...], wo[:, other_cols])
    unit_one, scale_one = norm(x_ref[...].astype(F32) + attn + vec_ref[0:1, :])
    middle = unit_one * vec_ref[1:2, :] + vec_ref[2:3, :]
    mlow_ref[...] = middle.astype(BF16)
    acc[...] = middle + vec_ref[3:4, :]

    @pl.loop(0, chunks)
    def _(k):
        place = pl.ds(pl.multiple_of(k * units, units), units)
        upper = mm(mlow_ref[...], ww[k, :, :units]) + upb_ref[:, place]
        active, rise = gelu_parts(upper)
        active = active.astype(BF16)
        act_ref[:, place] = active
        slope[:, place] = rise.astype(BF16)
        acc[...] += mm_rt(active, ww[k, :, units:])

    unit_two, scale_two = norm(acc[...])
    gain_two = vec_ref[4:5, :]
    layer_ref[...] = (unit_two * gain_two + vec_ref[5:6, :]).astype(BF16)
    cot = cot_ref[...].astype(F32)
    grad_two = norm_back(cot, unit_two, scale_two, gain_two)
    sums_ref[4:5, :] += jnp.sum(cot * unit_two, axis=0, keepdims=True)
    sums_ref[5:6, :] += jnp.sum(cot, axis=0, keepdims=True)
    sums_ref[3:4, :] += jnp.sum(grad_two, axis=0, keepdims=True)
    gb_ref[...] = grad_two.astype(BF16)
    acc[...] = grad_two

    @pl.loop(0, chunks)
    def _(k):
        place = pl.ds(pl.multiple_of(k * units, units), units)
        grad_upper = mm(gb_ref[...], ww[k, :, units:]) * slope[:, place].astype(F32)
        upsum_ref[:, place] += jnp.sum(grad_upper, axis=0, keepdims=True)
        grad_low = grad_upper.astype(BF16)
        gul_ref[:, place] = grad_low
        acc[...] += mm_rt(grad_low, ww[k, :, :units])

    grad_mid = acc[...]
    sums_ref[1:2, :] += jnp.sum(grad_mid * unit_one, axis=0, keepdims=True)
    sums_ref[2:3, :] += jnp.sum(grad_mid, axis=0, keepdims=True)
    grad_one = norm_back(grad_mid, unit_one, scale_one, vec_ref[1:2, :])
    sums_ref[0:1, :] += jnp.sum(grad_one, axis=0, keepdims=True)
    gone_ref[...] = grad_one
    grad_attn = grad_one.astype(BF16)
    ga_ref[...] = grad_attn
    gm_mine[...] = mm(grad_attn, wo[:, mine_cols]).astype(BF16)
    gm_other[...] = mm(grad_attn, wo[:, other_cols]).astype(BF16)


def dense(place, o_pieces, w_pieces, x, mine, other, cot, vec, upb, tile):
    count, width = x.shape
    cols = other.shape[1]
    chunks, units = w_pieces[0].shape[0], w_pieces[0].shape[2] // 2
    rows = lambda n: pl.BlockSpec((tile, n), lambda i, p: (i, 0))
    fixed = lambda a, b: pl.BlockSpec((a, b), lambda i, p: (0, 0))
    full = chunks * units
    shapes = [
        ((count, width), BF16), ((count, cols), BF16), ((count, cols), BF16), ((count, full), BF16),
        ((count, width), BF16), ((count, width), BF16), ((count, full), BF16), ((count, width), BF16),
        ((count, width), F32), ((8, width), F32), ((1, full), F32),
    ]
    flops = 8 * count * width * full + 4 * count * width * 2 * cols
    return pl.pallas_call(
        functools.partial(dense_kernel, n_o=len(o_pieces), n_w=len(w_pieces), chunks=chunks),
        grid_spec=pltpu.PrefetchScalarGridSpec(
            num_scalar_prefetch=1,
            grid=(count // tile,),
            in_specs=[ANY] * (len(o_pieces) + len(w_pieces))
            + [rows(width), rows(cols), rows(cols), rows(width), fixed(8, width), fixed(1, full)],
            out_specs=[
                rows(width), rows(cols), rows(cols), rows(full), rows(width), rows(width), rows(full),
                rows(width), rows(width), fixed(8, width), fixed(1, full),
            ],
            scratch_shapes=[
                pltpu.VMEM((width, 2 * cols), BF16),
                pltpu.VMEM((chunks, width, 2 * units), BF16),
                pltpu.VMEM((tile, full), BF16),
                pltpu.VMEM((tile, width), F32),
                pltpu.SemaphoreType.DMA((len(o_pieces) + len(w_pieces),)),
            ],
        ),
        out_shape=[jax.ShapeDtypeStruct(*s) for s in shapes],
        compiler_params=pltpu.CompilerParams(vmem_limit_bytes=LIMIT),
        cost_estimate=pl.CostEstimate(flops=flops, bytes_accessed=40 << 20, transcendentals=0),
        name="dense",
    )(place, *o_pieces, *w_pieces, x, mine, other, cot, vec, upb)


def grad_kernel(place_ref, *refs, n_r, drows, pairs):
    left_ref, right_refs, (ours_ref, theirs_ref, left_t, acc) = refs[0], refs[1 : 1 + n_r], refs[1 + n_r :]
    core = place_ref[0] % 2

    @pl.when(pl.program_id(0) == 0)
    def _():
        left_t[...] = left_ref[...].T

    if n_r == 1:
        acc[...] = mm(left_t[...], right_refs[0][...])
    else:
        cols = right_refs[0].shape[1]
        mine_cols = pl.ds(pl.multiple_of(core * cols, cols), cols)
        other_cols = pl.ds(pl.multiple_of((1 - core) * cols, cols), cols)
        acc[:, mine_cols] = mm(left_t[...], right_refs[0][...])
        acc[:, other_cols] = mm(left_t[...], right_refs[1][...])
    for p in range(pairs):
        ours_ref[p] = acc[pl.ds(pl.multiple_of((2 * p + core) * drows, drows), drows), :]
        theirs_ref[p] = acc[pl.ds(pl.multiple_of((2 * p + 1 - core) * drows, drows), drows), :].astype(BF16)


def weight_grad(place, left, rights, drows, tile):
    width, pairs = left.shape[1], left.shape[1] // (2 * drows)
    count = left.shape[0]
    if drows % 8:
        right = rights[0]
        if len(rights) > 1:
            right = jnp.where(
                place[0] % 2 == 0,
                jnp.concatenate([rights[0][:count], rights[1]], axis=1),
                jnp.concatenate([rights[1], rights[0][:count]], axis=1),
            )
        view = mm_lt(left, right).reshape(pairs, 2, drows, right.shape[1])
        ours = lax.dynamic_index_in_dim(view, place[0] % 2, 1, keepdims=False)
        theirs = lax.dynamic_index_in_dim(view, 1 - place[0] % 2, 1, keepdims=False)
        return ours, theirs.astype(BF16)
    cols = sum(r.shape[1] for r in rights)
    if len(rights) > 1:
        tile = cols
    block = tile // len(rights)
    return pl.pallas_call(
        functools.partial(grad_kernel, n_r=len(rights), drows=drows, pairs=pairs),
        grid_spec=pltpu.PrefetchScalarGridSpec(
            num_scalar_prefetch=1,
            grid=(cols // tile,),
            in_specs=[pl.BlockSpec((count, width), lambda i, p: (0, 0))]
            + [pl.BlockSpec((count, block), lambda i, p: (0, i))] * len(rights),
            out_specs=[pl.BlockSpec((pairs, drows, tile), lambda i, p: (0, 0, i))] * 2,
            scratch_shapes=[pltpu.VMEM((width, count), BF16), pltpu.VMEM((width, tile), F32)],
        ),
        out_shape=[
            jax.ShapeDtypeStruct((pairs, drows, cols), F32),
            jax.ShapeDtypeStruct((pairs, drows, cols), BF16),
        ],
        compiler_params=pltpu.CompilerParams(vmem_limit_bytes=LIMIT),
        cost_estimate=pl.CostEstimate(
            flops=2 * count * width * cols, bytes_accessed=8 * width * cols, transcendentals=0
        ),
        name="weight_grad",
    )(place, left, *rights)


def xor_order(parts, index):
    parts = list(parts)
    bit = 1
    while bit < len(parts):
        odd = (index // bit) % 2 == 1
        parts = [jnp.where(odd, parts[k ^ bit], parts[k]) for k in range(len(parts))]
        bit *= 2
    return parts


def per_device(
    tokens,
    segments,
    pairing,
    qkv_weight,
    qv_bias,
    out_weight,
    out_bias,
    first_gain,
    first_shift,
    up_weight,
    up_bias,
    down_weight,
    down_bias,
    second_gain,
    second_shift,
    cotangent,
):
    width = tokens.shape[2]
    rows = tokens.shape[1]
    lheads, blocks = pairing.shape
    hs = qv_bias.shape[1] // 2
    lanes = 2 * hs
    units = up_weight.shape[1]
    ndp, nt = lax.axis_size("dp"), lax.axis_size("tensor")
    drows = width // ndp
    chips = ndp // 2
    dp, tensor = lax.axis_index("dp"), lax.axis_index("tensor")
    core, chip, half, low = dp % 2, dp // 2, tensor // 2, tensor % 2
    slot_mask = 2 * core + low
    heads = 2 * lheads
    cols = heads * hs
    aligned = drows % 8 == 0
    place = jnp.stack([dp, tensor]).astype(jnp.int32)
    order = [0, 1, 3, 4, 2, 5]

    core_pairs = [(i, i ^ 1) for i in range(ndp)]

    def core_swap(x):
        return lax.ppermute(x, "dp", core_pairs)

    def z_step(x, k):
        return lax.ppermute(x, "tensor", [(i, i ^ k) for i in range(nt)])

    def chip_step(x, k):
        return lax.ppermute(x, "dp", [(i, i ^ (2 * k)) for i in range(ndp)])

    def column(k, flip, back):
        steps = []
        for p in range(chips):
            for c in range(2):
                for a in range(2):
                    for b in range(2):
                        home = (2 * p + c) * nt + 2 * a + b
                        away = (2 * p + (a ^ flip)) * nt + 2 * c + (b ^ k)
                        steps.append((away, home) if back else (home, away))
        return steps

    def to_sequence(x):
        return [
            lax.ppermute(
                lax.dynamic_index_in_dim(x, low ^ k, 0, keepdims=False), BOTH, column(k, 0, False)
            )
            for k in range(2)
        ]

    def to_home(parts):
        first, second = [lax.ppermute(parts[k], BOTH, column(k, 0, True)) for k in range(2)]
        return jnp.stack([jnp.where(low == 0, first, second), jnp.where(low == 0, second, first)])

    def z_all(x):
        return [x] + [z_step(x, k) for k in range(1, nt)]

    def chip_all(x):
        return [x] + [chip_step(x, k) for k in range(1, chips)]

    small = jnp.concatenate([pairing.astype(BF16).reshape(-1), qv_bias.reshape(-1), up_bias])
    n_pair, n_qv = lheads * blocks, lheads * lanes
    small_rel = z_all(small)
    small = jnp.stack(xor_order(small_rel, tensor))
    all_pairs = small[:, :n_pair].astype(jnp.int32).reshape(2, heads, blocks)
    my_pairs = jnp.where(core == 0, all_pairs[0], all_pairs[1])
    pair_slots = jnp.stack(xor_order([my_pairs[:, k] for k in range(blocks)], slot_mask), axis=1) ^ slot_mask
    pair_slots = jnp.stack([pair_slots[h] for h in order])
    all_qvb = small[:, n_pair : n_pair + n_qv].astype(F32).reshape(2, heads, lanes)
    my_qvb = jnp.where(core == 0, all_qvb[0], all_qvb[1])
    my_qvb = jnp.stack([my_qvb[h] for h in order])
    up_bias_rel = jnp.concatenate([s[n_pair + n_qv :] for s in small_rel]).astype(F32)
    groups = heads // 2
    bias = jnp.concatenate(
        [
            my_qvb[:, :hs].reshape(groups, lanes),
            jnp.zeros((groups, lanes), F32),
            my_qvb[:, hs:].reshape(groups, lanes),
        ],
        axis=1,
    ).reshape(groups, 1, 3 * lanes)

    segs = jnp.where(half == core, segments, core_swap(segments))
    seg_rows = jnp.where(low == 0, segs[0], segs[1]).reshape(blocks, rows)
    seg_row = jnp.concatenate(xor_order([seg_rows[k] for k in range(blocks)], slot_mask))
    seg_col = seg_row.reshape(blocks * rows, 1)
    seg_row = seg_row.reshape(1, blocks * rows)

    qkv_local = qkv_weight.reshape(drows, lheads, 3, hs).transpose(0, 2, 1, 3)
    qkv_local = jnp.concatenate(
        [qkv_local[:, :, :2].reshape(drows, 3 * lanes), qkv_local[:, :, 2].reshape(drows, 3 * hs)], axis=1
    )
    qkv_abs = xor_order(z_all(qkv_local), tensor)

    def regroup(first, second):
        left, right = first[:, 3 * lanes :], second[:, 3 * lanes :]
        both = [part[:, hs * k : hs * (k + 1)] for k in range(3) for part in (left, right)]
        return jnp.stack([first[:, : 3 * lanes], second[:, : 3 * lanes], jnp.concatenate(both, axis=1)])

    zero_heads, one_heads = regroup(qkv_abs[0], qkv_abs[1]), regroup(qkv_abs[2], qkv_abs[3])
    keep = jnp.where(core == 0, zero_heads, one_heads)
    got = core_swap(jnp.where(core == 0, one_heads, zero_heads))
    chip_rows = jnp.where(
        core == 0, jnp.concatenate([keep, got], axis=1), jnp.concatenate([got, keep], axis=1)
    )
    qkv_pieces = chip_all(chip_rows)
    if not aligned:
        qkv_pieces = [jnp.concatenate(xor_order(qkv_pieces, chip), axis=1)]

    mine = to_sequence(tokens)
    x_parts = mine + [core_swap(part) for part in mine]
    x_mine = jnp.concatenate(mine)

    out_abs = xor_order(z_all(out_weight.reshape(lheads * hs, drows).T), tensor)
    out_cols = []
    for u in range(2):
        first, second = out_abs[2 * u], out_abs[2 * u + 1]
        out_cols += [first[:, :lanes], second[:, :lanes], first[:, lanes:], second[:, lanes:]]
    out_own = chip_all(jnp.concatenate(out_cols, axis=1))
    out_pieces = [part for own in out_own for part in (own, core_swap(own))]

    ff_own = chip_all(jnp.stack(z_all(jnp.concatenate([up_weight, down_weight.T], axis=1))))
    ff_pieces = [part for own in ff_own for part in (own, core_swap(own))]
    if not aligned:
        out_pieces = [jnp.concatenate(xor_order(out_pieces, dp))]
        ff_pieces = [jnp.concatenate(xor_order(ff_pieces, dp), axis=1)]
    upstream = jnp.concatenate(to_sequence(cotangent))

    q, k, v, mixed, lse = attend(pair_slots, place, x_parts, qkv_pieces, bias, seg_row, seg_col, hs)
    count = blocks // 2 * rows
    other = core_swap(mixed[count:])

    blank = jnp.zeros((width,), BF16)
    vec = jnp.stack(
        [out_bias, first_gain, first_shift, down_bias, second_gain, second_shift, blank, blank]
    ).astype(F32)
    (
        layer_mine, gm_mine, gm_other, active, middle_low, grad_branch, grad_upper, grad_attn, grad_one, sums, up_sums,
    ) = dense(
        place, out_pieces, ff_pieces, x_mine, mixed, other, upstream, vec, up_bias_rel.reshape(1, nt * units), 256
    )
    layer_out = to_home([layer_mine[:rows], layer_mine[rows:]])

    def reduce_plane(view):
        total = lax.dynamic_index_in_dim(view, chip, 0, keepdims=False)
        for k in range(1, chips):
            part = lax.dynamic_index_in_dim(view, chip ^ k, 0, keepdims=False).astype(BF16)
            total = total + chip_step(part, k).astype(F32)
        return total

    def reduce_weight(left, rights):
        ours, theirs = weight_grad(place, left, rights, drows, 512)
        return reduce_plane(ours + core_swap(theirs).astype(F32))

    def reduce_relative(grad):
        total = grad[:, :units]
        for k in range(1, nt):
            part = grad[:, units * k : units * (k + 1)].astype(BF16)
            total = total + z_step(part, k).astype(F32)
        return total

    down_grad = reduce_relative(reduce_weight(grad_branch, [active])).T
    up_grad = reduce_relative(reduce_weight(middle_low, [grad_upper]))
    out_sum = reduce_weight(grad_attn, [mixed, other])
    out_parts = []
    for u in range(2):
        base = u * cols
        for w in range(2):
            out_parts.append(
                jnp.concatenate(
                    [
                        out_sum[:, base + lanes * w : base + lanes * (w + 1)],
                        out_sum[:, base + 2 * lanes + hs * w : base + 2 * lanes + hs * (w + 1)],
                    ],
                    axis=1,
                )
            )
    out_rel = xor_order(out_parts, tensor)
    out_grad = out_rel[0]
    for step in range(1, nt):
        out_grad = out_grad + z_step(out_rel[step].astype(BF16), step).astype(F32)
    out_grad = out_grad.T.reshape(lheads, hs, drows)

    def all_sum(x):
        for bit in range(nt.bit_length() - 1):
            x = x + z_step(x, 1 << bit)
        for bit in range(ndp.bit_length() - 1):
            x = x + lax.ppermute(x, "dp", [(i, i ^ (1 << bit)) for i in range(ndp)])
        return x

    up_abs = xor_order([up_sums[0, units * k : units * (k + 1)] for k in range(nt)], tensor)
    sums = all_sum(jnp.concatenate([sums[:6].reshape(-1)] + up_abs))
    outb_grad, gain_one_grad, shift_one_grad, downb_grad, gain_two_grad, shift_two_grad = [
        sums[i * width : (i + 1) * width] for i in range(6)
    ]
    upb_grad = lax.dynamic_slice(sums, (6 * width + tensor * units,), (units,))

    gm_all = jnp.concatenate([gm_mine, core_swap(gm_other)])
    qkv_part, in_mine, in_other, head_sums = attend_back(
        pair_slots, place, x_parts, qkv_pieces, q, k, v, gm_all, seg_row, seg_col, lse, hs
    )
    in_low = (in_mine + core_swap(in_other).astype(F32) + grad_one).astype(BF16)
    input_grad = to_home([in_low[:rows], in_low[rows:]])

    view = qkv_part.reshape(groups, chips, 2 * drows, 3 * lanes).transpose(1, 0, 2, 3)
    qkv_sum = reduce_plane(view).reshape(groups, 2, drows, 3 * lanes)

    def share(c, u):
        third = [qkv_sum[2, c][:, lanes * k + hs * u : lanes * k + hs * (u + 1)] for k in range(3)]
        return jnp.concatenate([qkv_sum[u, c]] + third, axis=1)

    shares = [[share(c, u).astype(BF16) for u in range(2)] for c in range(2)]
    qkv_grad = jnp.zeros((drows, 3 * lheads * hs), F32)
    for flip in range(2):
        for step in range(2):
            by_core = [jnp.where((low ^ step) == 0, shares[c][0], shares[c][1]) for c in range(2)]
            sent = jnp.where((half ^ flip) == 0, by_core[0], by_core[1])
            qkv_grad = qkv_grad + lax.ppermute(sent, BOTH, column(step, flip, False)).astype(F32)
    pairs_part = qkv_grad[:, : 3 * lanes].reshape(drows, 3, 2, hs)
    third_part = qkv_grad[:, 3 * lanes :].reshape(drows, 3, 1, hs)
    qkv_grad = jnp.concatenate([pairs_part, third_part], axis=2).transpose(0, 2, 1, 3)
    qkv_grad = qkv_grad.reshape(drows, lheads, 3 * hs)

    q_sum = head_sums[:, 0, :].reshape(heads, hs)
    v_sum = head_sums[:, 1, :].reshape(heads, hs)
    own_qvb = jnp.concatenate([q_sum, v_sum], axis=1)
    own_qvb = jnp.stack([own_qvb[order.index(h)] for h in range(heads)])
    blank = jnp.zeros_like(own_qvb)
    both = jnp.concatenate([jnp.where(core == 0, own_qvb, blank), jnp.where(core == 0, blank, own_qvb)])
    both = all_sum(both)
    qvb_grad = lax.dynamic_slice(both, (tensor * lheads, 0), (lheads, lanes))
    return (
        layer_out,
        input_grad,
        qkv_grad,
        qvb_grad,
        out_grad,
        outb_grad,
        gain_one_grad,
        shift_one_grad,
        up_grad,
        upb_grad,
        down_grad,
        downb_grad,
        gain_two_grad,
        shift_two_grad,
    )


def solution(mesh):
    return jax.shard_map(
        per_device,
        mesh=mesh,
        in_specs=(
            P("dp", "tensor", None),
            P("dp", None),
            P("tensor", None),
            P("dp", "tensor", None),
            P("tensor", None),
            P("tensor", None, "dp"),
            P(),
            P(),
            P(),
            P("dp", "tensor"),
            P("tensor"),
            P("tensor", "dp"),
            P(),
            P(),
            P(),
            P("dp", "tensor", None),
        ),
        out_specs=(
            P("dp", "tensor", None),
            P("dp", "tensor", None),
            P("dp", "tensor", None),
            P("tensor", None),
            P("tensor", None, "dp"),
            P(),
            P(),
            P(),
            P("dp", "tensor"),
            P("tensor"),
            P("tensor", "dp"),
            P(),
            P(),
            P(),
        ),
        check_vma=False,
    )
```

profile of v0, /device:TPU:0, one launch (start us, length us, event | category | flops | bytes accessed | tf_op | source)
XLA Modules:
  0.0 487.7 jit_solution(4000456561970702892)
XLA Ops:
  2.0 5.1 %collective-permute-start.27 = (bf16[96,576]{1,0:T(8,128)(2,1)S(1)}, bf16[96,576]{1,0:T(8,128)(2,1)S(1)}, u32[]{:S(2)}, u32[]{:S(2)}) collective-permute-start(bf16[96,576]{1,0:T(8,128)(2,1)S(1)} %pad_maximum_fusion.9), channel_id=1, source_target_pairs={{0,3},{1,2},{2,1},{3,0},{4,7},{5,6},{6,5},{7,4},{8,11},{9,10},{10,... | collective-permute-start | bytes 331784 | tf_op jit(solution)/shard_map/ppermute | solution.py:532
  13.8 2.7 dynamic-slice_bitcast_fusion.3
  19.3 2.9 collective-permute-start
  33.7 3.4 collective-permute-start.11
  40.5 16.0 %collective-permute-done.11 = bf16[96,1536]{1,0:T(8,128)(2,1)S(1)} collective-permute-done((bf16[96,1536]{1,0:T(8,128)(2,1)S(1)}, bf16[96,1536]{1,0:T(8,128)(2,1)S(1)}, u32[]{:S(2)}, u32[]{:S(2)}) %collective-permute-start.11) | collective-permute-done | bytes 294944 | tf_op jit(solution)/shard_map/ppermute | solution.py:532
  58.3 3.5 collective-permute-start.21
  61.7 7.4 %collective-permute-start.36 = (bf16[512,768]{1,0:T(8,128)(2,1)}, bf16[512,768]{1,0:T(8,128)(2,1)}, u32[]{:S(2)}, u32[]{:S(2)}) collective-permute-start(bf16[512,768]{1,0:T(8,128)(2,1)} %get-tuple-element.135), channel_id=1, source_target_pairs={{0,0},{1,1},{2,4},{3,5},{4,2},{5,3},{6,6},{7,7},{8,8},{9,9},{10,12... | collective-permute-start | bytes 2359304 | tf_op jit(solution)/shard_map/ppermute | solution.py:550
  76.8 15.6 %collective-permute-done.32.refs_6_ = bf16[3,192,384]{2,1,0:T(8,128)(2,1)S(1)} collective-permute-done((bf16[3,192,384]{2,1,0:T(8,128)(2,1)S(1)}, bf16[3,192,384]{2,1,0:T(8,128)(2,1)S(1)}, u32[]{:S(2)}, u32[]{:S(2)}) %collective-permute-start.32) | collective-permute-done | bytes 442400 | tf_op jit(solution)/shard_map/ppermute | solution.py:535
  96.0 15.6 %collective-permute-start.26 = (bf16[512,768]{1,0:T(8,128)(2,1)S(1)}, bf16[512,768]{1,0:T(8,128)(2,1)}, u32[]{:S(2)}, u32[]{:S(2)}) collective-permute-start(bf16[512,768]{1,0:T(8,128)(2,1)S(1)} %collective-permute-done.21.refs_1_), channel_id=1, source_target_pairs={{0,4},{4,0},{8,12},{12,8},{16,20},{20,16},{24,28},{28,24},{1,5},{5... | collective-permute-start | bytes 2359304 | tf_op jit(solution)/shard_map/ppermute | solution.py:529
  113.1 8.4 %collective-permute-done.14.refs_10_ = bf16[4,96,1536]{2,1,0:T(8,128)(2,1)} collective-permute-done((bf16[4,96,1536]{2,1,0:T(8,128)(2,1)S(1)}, bf16[4,96,1536]{2,1,0:T(8,128)(2,1)}, u32[]{:S(2)}, u32[]{:S(2)}) %collective-permute-start.14) | collective-permute-done | bytes 1179680 | tf_op jit(solution)/shard_map/ppermute | solution.py:535
  122.0 24.3 %collective-permute-done.16.refs_12_ = bf16[4,96,1536]{2,1,0:T(8,128)(2,1)} collective-permute-done((bf16[4,96,1536]{2,1,0:T(8,128)(2,1)S(1)}, bf16[4,96,1536]{2,1,0:T(8,128)(2,1)}, u32[]{:S(2)}, u32[]{:S(2)}) %collective-permute-start.16) | collective-permute-done | bytes 1179680 | tf_op jit(solution)/shard_map/ppermute | solution.py:535
  147.3 27.5 %attend.1 = (bf16[2048,384]{1,0:T(8,128)(2,1)}, bf16[2048,384]{1,0:T(8,128)(2,1)}, bf16[2048,384]{1,0:T(8,128)(2,1)}, bf16[2048,384]{1,0:T(8,128)(2,1)}, f32[3,8,2048]{2,1,0:T(8,128)}) custom-call(s32[6,4]{1,0:T(8,128)} %pad_add_fusion.1.pair_ref, s32[2]{0:T(128)} %pad_add_fusion.2.place_ref, bf16[512,768]{1,0:T(8,128)(2,1)} %copy-done.5, ...), custom_call_target="tpu_custom_call" | custom-call | flops 10066329600 | bytes 20971520 | tf_op jit(solution)/shard_map/attend/pallas_call | solution.py:115
  183.8 54.0 %dense.1 = (bf16[1024,768]{1,0:T(8,128)(2,1)}, bf16[1024,384]{1,0:T(8,128)(2,1)}, bf16[1024,384]{1,0:T(8,128)(2,1)}, bf16[1024,3072]{1,0:T(8,128)(2,1)}, bf16[10...) custom-call(s32[2]{0:T(128)} %pad_add_fusion.2.place_ref, ...), custom_call_target="tpu_custom_call" | custom-call | flops 21743271936 | bytes 41943040 | tf_op jit(solution)/shard_map/dense/pallas_call | solution.py:392
  240.1 3.2 collective-permute-done.63
  244.4 5.8 %weight_grad.3 = (f32[4,96,768]{2,1,0:T(8,128)}, bf16[4,96,768]{2,1,0:T(8,128)(2,1)}) custom-call(s32[2]{0:T(128)} %pad_add_fusion.2.place_ref, bf16[1024,768]{1,0:T(8,128)(2,1)} %get-tuple-element.53.refs_0_, bf16[2048,384]{1,0:T(8,128)(2,1)} %get-tuple-element.40.refs_17_.refs_1_, bf16[1024,384]{1,0:T(8,128)(2,1)} %collective-permute-done.35.refs_18_.refs_2_), custom_call_target="tpu_custom_call" | custom-call | flops 1207959552 | bytes 4718592 | tf_op jit(solution)/shard_map/weight_grad/pallas_call | solution.py:458
  253.2 11.9 %weight_grad.5 = (f32[4,96,3072]{2,1,0:T(8,128)}, bf16[4,96,3072]{2,1,0:T(8,128)(2,1)}) custom-call(s32[2]{0:T(128)} %pad_add_fusion.2.place_ref, bf16[1024,768]{1,0:T(8,128)(2,1)} %get-tuple-element.62.refs_0_, bf16[1024,3072]{1,0:T(8,128)(2,1)} %get-tuple-element.63.refs_1_), custom_call_target="tpu_custom_call" | custom-call | flops 4831838208 | bytes 18874368 | tf_op jit(solution)/shard_map/weight_grad/pallas_call | solution.py:458
  266.3 12.0 %weight_grad.4 = (f32[4,96,3072]{2,1,0:T(8,128)}, bf16[4,96,3072]{2,1,0:T(8,128)(2,1)}) custom-call(s32[2]{0:T(128)} %pad_add_fusion.2.place_ref, bf16[1024,768]{1,0:T(8,128)(2,1)} %get-tuple-element.58.refs_0_, bf16[1024,3072]{1,0:T(8,128)(2,1)} %get-tuple-element.59.refs_1_), custom_call_target="tpu_custom_call" | custom-call | flops 4831838208 | bytes 18874368 | tf_op jit(solution)/shard_map/weight_grad/pallas_call | solution.py:458
  284.2 3.2 collective-permute-start.39
  296.9 47.7 %attend_back.1 = (f32[3,768,384]{2,1,0:T(8,128)}, f32[1024,768]{1,0:T(8,128)}, bf16[1024,768]{1,0:T(8,128)(2,1)}, f32[3,8,128]{2,1,0:T(8,128)}) custom-call(s32[6,4]{1,0:T(8,128)} %pad_add_fusion.1.pair_ref, s32[2]{0:T(128)} %pad_add_fusion.2.place_ref, bf16[512,768]{1,0:T(8,128)(2,1)} %copy-done.5, bf16[512,768]{1,0:T(8,128)(2,1)} %copy-done.7, ...), custom_call_target="tpu_custom_call" | custom-call | flops 23353884672 | bytes 31457280 | tf_op jit(solution)/shard_map/attend_back/pallas_call | solution.py:233
  361.2 15.0 %collective-permute-done.54 = f32[12,128]{1,0:T(8,128)S(1)} collective-permute-done((f32[12,128]{1,0:T(8,128)S(1)}, f32[12,128]{1,0:T(8,128)S(1)}, u32[]{:S(2)}, u32[]{:S(2)}) %collective-permute-start.54) | collective-permute-done | bytes 6176 | tf_op jit(solution)/shard_map/ppermute | solution.py:693
  380.9 3.5 collective-permute-start.49
  387.3 5.0 %collective-permute-start.68 = (bf16[4,96,3072]{2,1,0:T(8,128)(2,1)}, bf16[4,96,3072]{2,1,0:T(8,128)(2,1)}, u32[]{:S(2)}, u32[]{:S(2)}) collective-permute-start(bf16[4,96,3072]{2,1,0:T(8,128)(2,1)} %get-tuple-element.61), channel_id=1, source_target_pairs={{0,4},{4,0},{8,12},{12,8},{16,20},{20,16},{24,28},{28,24},{1,5},{5... | collective-permute-start | bytes 7077896 | tf_op jit(solution)/shard_map/ppermute | solution.py:529
  397.4 3.1 add_convert_fusion
  403.3 2.7 convert_add_fusion
  412.7 9.6 %collective-permute-done.76 = bf16[96,3072]{1,0:T(8,128)(2,1)S(1)} collective-permute-done((bf16[96,3072]{1,0:T(8,128)(2,1)S(1)}, bf16[96,3072]{1,0:T(8,128)(2,1)S(1)}, u32[]{:S(2)}, u32[]{:S(2)}) %collective-permute-start.76) | collective-permute-done | bytes 589856 | tf_op jit(solution)/shard_map/ppermute | solution.py:535
  422.9 12.1 %collective-permute-done.77 = bf16[96,3072]{1,0:T(8,128)(2,1)S(1)} collective-permute-done((bf16[96,3072]{1,0:T(8,128)(2,1)S(1)}, bf16[96,3072]{1,0:T(8,128)(2,1)S(1)}, u32[]{:S(2)}, u32[]{:S(2)}) %collective-permute-start.77) | collective-permute-done | bytes 589856 | tf_op jit(solution)/shard_map/ppermute | solution.py:535
  435.0 3.6 collective-permute-start.71
  439.0 8.6 %collective-permute-done.69 = bf16[96,3072]{1,0:T(8,128)(2,1)S(1)} collective-permute-done((bf16[96,3072]{1,0:T(8,128)(2,1)S(1)}, bf16[96,3072]{1,0:T(8,128)(2,1)S(1)}, u32[]{:S(2)}, u32[]{:S(2)}) %collective-permute-start.69) | collective-permute-done | bytes 589856 | tf_op jit(solution)/shard_map/ppermute | solution.py:535
  447.6 15.3 %collective-permute-done.70 = bf16[96,3072]{1,0:T(8,128)(2,1)S(1)} collective-permute-done((bf16[96,3072]{1,0:T(8,128)(2,1)S(1)}, bf16[96,3072]{1,0:T(8,128)(2,1)S(1)}, u32[]{:S(2)}, u32[]{:S(2)}) %collective-permute-start.70) | collective-permute-done | bytes 589856 | tf_op jit(solution)/shard_map/ppermute | solution.py:535
  463.2 3.5 collective-permute-start.72
  466.8 7.7 %collective-permute-done.80 = bf16[96,768]{1,0:T(8,128)(2,1)S(1)} collective-permute-done((bf16[96,768]{1,0:T(8,128)(2,1)S(1)}, bf16[96,768]{1,0:T(8,128)(2,1)S(1)}, u32[]{:S(2)}, u32[]{:S(2)}) %collective-permute-start.80) | collective-permute-done | bytes 147488 | tf_op jit(solution)/shard_map/ppermute | solution.py:532
  475.4 10.2 %collective-permute-done.73 = bf16[96,768]{1,0:T(8,128)(2,1)S(1)} collective-permute-done((bf16[96,768]{1,0:T(8,128)(2,1)S(1)}, bf16[96,768]{1,0:T(8,128)(2,1)S(1)}, u32[]{:S(2)}, u32[]{:S(2)}) %collective-permute-start.73) | collective-permute-done | bytes 147488 | tf_op jit(solution)/shard_map/ppermute | solution.py:532
  (375 shorter events, 115.7 us)
Async XLA Ops:
  33.7 22.8 %collective-permute-start.11 = (bf16[96,1536]{1,0:T(8,128)(2,1)S(1)}, bf16[96,1536]{1,0:T(8,128)(2,1)S(1)}, u32[]{:S(2)}, u32[]{:S(2)}) collective-permute-start(bf16[96,1536]{1,0:T(8,128)(2,1)S(1)} %get-tuple-element.171), channel_id=1, source_target_pairs={{0,2},{1,3},{2,0},{3,1},{4,6},{5,7},{6,4},{7,5},{8,10},{9,11},{10,... | collective-permute-start | bytes 884744 | tf_op jit(solution)/shard_map/ppermute | solution.py:532
  39.7 29.4 %collective-permute-start.7 = (bf16[96,768]{1,0:T(8,128)(2,1)S(1)}, bf16[96,768]{1,0:T(8,128)(2,1)S(1)}, u32[]{:S(2)}, u32[]{:S(2)}) collective-permute-start(bf16[96,768]{1,0:T(8,128)(2,1)S(1)} %collective-permute-done.6.refs_4_), channel_id=1, source_target_pairs={{0,4},{4,0},{8,12},{12,8},{16,20},{20,16},{24,28},{28,24},{1,5},{5... | collective-permute-start | bytes 442376 | tf_op jit(solution)/shard_map/ppermute | solution.py:529
  40.4 31.9 %collective-permute-start.31 = (bf16[3,192,384]{2,1,0:T(8,128)(2,1)S(1)}, bf16[3,192,384]{2,1,0:T(8,128)(2,1)S(1)}, u32[]{:S(2)}, u32[]{:S(2)}) collective-permute-start(bf16[3,192,384]{2,1,0:T(8,128)(2,1)S(1)} %maximum_select_fusion.refs_4_), channel_id=1, source_target_pairs={{0,8},{4,12},{8,0},{12,4},{16,24},{20,28},{24,16},{28,20},{1,9},{5... | collective-permute-start | bytes 1327112 | tf_op jit(solution)/shard_map/ppermute | solution.py:535
  56.5 39.0 %collective-permute-start.20 = (bf16[512,768]{1,0:T(8,128)(2,1)}, bf16[512,768]{1,0:T(8,128)(2,1)S(1)}, u32[]{:S(2)}, u32[]{:S(2)}) collective-permute-start(bf16[512,768]{1,0:T(8,128)(2,1)} %get-tuple-element.137), channel_id=1, source_target_pairs={{0,0},{1,1},{2,4},{3,5},{4,2},{5,3},{6,6},{7,7},{8,8},{9,9},{10,12... | collective-permute-start | bytes 2359304 | tf_op jit(solution)/shard_map/ppermute | solution.py:550
  58.3 37.7 %collective-permute-start.21 = (bf16[512,768]{1,0:T(8,128)(2,1)}, bf16[512,768]{1,0:T(8,128)(2,1)S(1)}, u32[]{:S(2)}, u32[]{:S(2)}) collective-permute-start(bf16[512,768]{1,0:T(8,128)(2,1)} %get-tuple-element.138), channel_id=1, source_target_pairs={{0,1},{1,0},{2,5},{3,4},{4,3},{5,2},{6,7},{7,6},{8,9},{9,8},{10,13... | collective-permute-start | bytes 2359304 | tf_op jit(solution)/shard_map/ppermute | solution.py:550
  61.7 34.3 %collective-permute-start.36 = (bf16[512,768]{1,0:T(8,128)(2,1)}, bf16[512,768]{1,0:T(8,128)(2,1)}, u32[]{:S(2)}, u32[]{:S(2)}) collective-permute-start(bf16[512,768]{1,0:T(8,128)(2,1)} %get-tuple-element.135), channel_id=1, source_target_pairs={{0,0},{1,1},{2,4},{3,5},{4,2},{5,3},{6,6},{7,7},{8,8},{9,9},{10,12... | collective-permute-start | bytes 2359304 | tf_op jit(solution)/shard_map/ppermute | solution.py:550
  92.5 29.0 %collective-permute-start.14 = (bf16[4,96,1536]{2,1,0:T(8,128)(2,1)S(1)}, bf16[4,96,1536]{2,1,0:T(8,128)(2,1)}, u32[]{:S(2)}, u32[]{:S(2)}) collective-permute-start(bf16[4,96,1536]{2,1,0:T(8,128)(2,1)S(1)} %pad_maximum_fusion.5.refs_8_), channel_id=1, source_target_pairs={{0,8},{4,12},{8,0},{12,4},{16,24},{20,28},{24,16},{28,20},{1,9},{5... | collective-permute-start | bytes 3538952 | tf_op jit(solution)/shard_map/ppermute | solution.py:535
  94.0 52.3 %collective-permute-start.16 = (bf16[4,96,1536]{2,1,0:T(8,128)(2,1)S(1)}, bf16[4,96,1536]{2,1,0:T(8,128)(2,1)}, u32[]{:S(2)}, u32[]{:S(2)}) collective-permute-start(bf16[4,96,1536]{2,1,0:T(8,128)(2,1)S(1)} %pad_maximum_fusion.5.refs_8_), channel_id=1, source_target_pairs={{0,16},{4,20},{8,24},{12,28},{16,0},{20,4},{24,8},{28,12},{1,17},{... | collective-permute-start | bytes 3538952 | tf_op jit(solution)/shard_map/ppermute | solution.py:535
  95.5 50.8 %collective-permute-start.18 = (bf16[4,96,1536]{2,1,0:T(8,128)(2,1)S(1)}, bf16[4,96,1536]{2,1,0:T(8,128)(2,1)}, u32[]{:S(2)}, u32[]{:S(2)}) collective-permute-start(bf16[4,96,1536]{2,1,0:T(8,128)(2,1)S(1)} %pad_maximum_fusion.5.refs_8_), channel_id=1, source_target_pairs={{0,24},{4,28},{8,16},{12,20},{16,8},{20,12},{24,0},{28,4},{1,25},{... | collective-permute-start | bytes 3538952 | tf_op jit(solution)/shard_map/ppermute | solution.py:535
  96.0 50.8 %collective-permute-start.25 = (bf16[512,768]{1,0:T(8,128)(2,1)S(1)}, bf16[512,768]{1,0:T(8,128)(2,1)}, u32[]{:S(2)}, u32[]{:S(2)}) collective-permute-start(bf16[512,768]{1,0:T(8,128)(2,1)S(1)} %collective-permute-done.20.refs_0_), channel_id=1, source_target_pairs={{0,4},{4,0},{8,12},{12,8},{16,20},{20,16},{24,28},{28,24},{1,5},{5... | collective-permute-start | bytes 2359304 | tf_op jit(solution)/shard_map/ppermute | solution.py:529
  96.0 50.9 %collective-permute-start.26 = (bf16[512,768]{1,0:T(8,128)(2,1)S(1)}, bf16[512,768]{1,0:T(8,128)(2,1)}, u32[]{:S(2)}, u32[]{:S(2)}) collective-permute-start(bf16[512,768]{1,0:T(8,128)(2,1)S(1)} %collective-permute-done.21.refs_1_), channel_id=1, source_target_pairs={{0,4},{4,0},{8,12},{12,8},{16,20},{20,16},{24,28},{28,24},{1,5},{5... | collective-permute-start | bytes 2359304 | tf_op jit(solution)/shard_map/ppermute | solution.py:529
  121.5 54.8 %collective-permute-start.37 = (bf16[512,768]{1,0:T(8,128)(2,1)}, bf16[512,768]{1,0:T(8,128)(2,1)S(1)}, u32[]{:S(2)}, u32[]{:S(2)}) collective-permute-start(bf16[512,768]{1,0:T(8,128)(2,1)} %get-tuple-element.136), channel_id=1, source_target_pairs={{0,1},{1,0},{2,5},{3,4},{4,3},{5,2},{6,7},{7,6},{8,9},{9,8},{10,13... | collective-permute-start | bytes 2359304 | tf_op jit(solution)/shard_map/ppermute | solution.py:550
  146.3 37.4 %collective-permute-start.13 = (bf16[4,96,1536]{2,1,0:T(8,128)(2,1)S(1)}, bf16[4,96,1536]{2,1,0:T(8,128)(2,1)}, u32[]{:S(2)}, u32[]{:S(2)}) collective-permute-start(bf16[4,96,1536]{2,1,0:T(8,128)(2,1)S(1)} %pad_maximum_fusion.5.refs_8_), channel_id=1, source_target_pairs={{0,4},{4,0},{8,12},{12,8},{16,20},{20,16},{24,28},{28,24},{1,5},{5... | collective-permute-start | bytes 3538952 | tf_op jit(solution)/shard_map/ppermute | solution.py:529
  146.3 37.4 %collective-permute-start.15 = (bf16[4,96,1536]{2,1,0:T(8,128)(2,1)}, bf16[4,96,1536]{2,1,0:T(8,128)(2,1)}, u32[]{:S(2)}, u32[]{:S(2)}) collective-permute-start(bf16[4,96,1536]{2,1,0:T(8,128)(2,1)} %collective-permute-done.14.refs_10_), channel_id=1, source_target_pairs={{0,4},{4,0},{8,12},{12,8},{16,20},{20,16},{24,28},{28,24},{1,5},{5... | collective-permute-start | bytes 3538952 | tf_op jit(solution)/shard_map/ppermute | solution.py:529
  146.8 36.9 %collective-permute-start.17 = (bf16[4,96,1536]{2,1,0:T(8,128)(2,1)}, bf16[4,96,1536]{2,1,0:T(8,128)(2,1)}, u32[]{:S(2)}, u32[]{:S(2)}) collective-permute-start(bf16[4,96,1536]{2,1,0:T(8,128)(2,1)} %collective-permute-done.16.refs_12_), channel_id=1, source_target_pairs={{0,4},{4,0},{8,12},{12,8},{16,20},{20,16},{24,28},{28,24},{1,5},{5... | collective-permute-start | bytes 3538952 | tf_op jit(solution)/shard_map/ppermute | solution.py:529
  146.9 36.9 %collective-permute-start.19 = (bf16[4,96,1536]{2,1,0:T(8,128)(2,1)}, bf16[4,96,1536]{2,1,0:T(8,128)(2,1)}, u32[]{:S(2)}, u32[]{:S(2)}) collective-permute-start(bf16[4,96,1536]{2,1,0:T(8,128)(2,1)} %collective-permute-done.18.refs_14_), channel_id=1, source_target_pairs={{0,4},{4,0},{8,12},{12,8},{16,20},{20,16},{24,28},{28,24},{1,5},{5... | collective-permute-start | bytes 3538952 | tf_op jit(solution)/shard_map/ppermute | solution.py:529
  250.2 28.2 %collective-permute-start.56 = (bf16[4,96,768]{2,1,0:T(8,128)(2,1)}, bf16[4,96,768]{2,1,0:T(8,128)(2,1)S(1)}, u32[]{:S(2)}, u32[]{:S(2)}) collective-permute-start(bf16[4,96,768]{2,1,0:T(8,128)(2,1)} %get-tuple-element.55), channel_id=1, source_target_pairs={{0,4},{4,0},{8,12},{12,8},{16,20},{20,16},{24,28},{28,24},{1,5},{5... | collective-permute-start | bytes 1769480 | tf_op jit(solution)/shard_map/ppermute | solution.py:529
  250.2 44.0 %collective-permute-start.40 = (bf16[1024,384]{1,0:T(8,128)(2,1)}, bf16[1024,384]{1,0:T(8,128)(2,1)S(1)}, u32[]{:S(2)}, u32[]{:S(2)}) collective-permute-start(bf16[1024,384]{1,0:T(8,128)(2,1)} %get-tuple-element.46), channel_id=1, source_target_pairs={{0,4},{4,0},{8,12},{12,8},{16,20},{20,16},{24,28},{28,24},{1,5},{5... | collective-permute-start | bytes 2359304 | tf_op jit(solution)/shard_map/ppermute | solution.py:529
  251.0 105.5 %collective-permute-start.38 = (bf16[512,768]{1,0:T(8,128)(2,1)S(1)}, bf16[512,768]{1,0:T(8,128)(2,1)S(1)}, u32[]{:S(2)}, u32[]{:S(2)}) collective-permute-start(bf16[512,768]{1,0:T(8,128)(2,1)S(1)} %get-tuple-element.133), channel_id=1, source_target_pairs={{0,0},{1,1},{4,2},{5,3},{2,4},{3,5},{6,6},{7,7},{8,8},{9,9},{12,10... | collective-permute-start | bytes 2359304 | tf_op jit(solution)/shard_map/ppermute | solution.py:557
  284.2 74.0 %collective-permute-start.39 = (bf16[512,768]{1,0:T(8,128)(2,1)S(1)}, bf16[512,768]{1,0:T(8,128)(2,1)S(1)}, u32[]{:S(2)}, u32[]{:S(2)}) collective-permute-start(bf16[512,768]{1,0:T(8,128)(2,1)S(1)} %get-tuple-element.134), channel_id=1, source_target_pairs={{1,0},{0,1},{5,2},{4,3},{3,4},{2,5},{7,6},{6,7},{9,8},{8,9},{13,10... | collective-permute-start | bytes 2359304 | tf_op jit(solution)/shard_map/ppermute | solution.py:557
  290.0 56.3 %collective-permute-start.60 = (bf16[96,192]{1,0:T(8,128)(2,1)}, bf16[96,192]{1,0:T(8,128)(2,1)}, u32[]{:S(2)}, u32[]{:S(2)}) collective-permute-start(bf16[96,192]{1,0:T(8,128)(2,1)} %get-tuple-element.160), channel_id=1, source_target_pairs={{0,1},{1,0},{2,3},{3,2},{4,5},{5,4},{6,7},{7,6},{8,9},{9,8},{10,11... | collective-permute-start | bytes 110600 | tf_op jit(solution)/shard_map/ppermute | solution.py:532
  292.6 53.7 %collective-permute-start.61 = (bf16[96,192]{1,0:T(8,128)(2,1)}, bf16[96,192]{1,0:T(8,128)(2,1)}, u32[]{:S(2)}, u32[]{:S(2)}) collective-permute-start(bf16[96,192]{1,0:T(8,128)(2,1)} %get-tuple-element.161), channel_id=1, source_target_pairs={{0,2},{1,3},{2,0},{3,1},{4,6},{5,7},{6,4},{7,5},{8,10},{9,11},{10,... | collective-permute-start | bytes 110600 | tf_op jit(solution)/shard_map/ppermute | solution.py:532
  294.3 53.2 %collective-permute-start.62 = (bf16[96,192]{1,0:T(8,128)(2,1)}, bf16[96,192]{1,0:T(8,128)(2,1)}, u32[]{:S(2)}, u32[]{:S(2)}) collective-permute-start(bf16[96,192]{1,0:T(8,128)(2,1)} %select_convert_fusion), channel_id=1, source_target_pairs={{0,3},{1,2},{2,1},{3,0},{4,7},{5,6},{6,5},{7,4},{8,11},{9,10},{10,... | collective-permute-start | bytes 110600 | tf_op jit(solution)/shard_map/ppermute | solution.py:532
  346.3 57.0 %collective-permute-start.75 = (bf16[4,96,3072]{2,1,0:T(8,128)(2,1)}, bf16[4,96,3072]{2,1,0:T(8,128)(2,1)}, u32[]{:S(2)}, u32[]{:S(2)}) collective-permute-start(bf16[4,96,3072]{2,1,0:T(8,128)(2,1)} %get-tuple-element.65), channel_id=1, source_target_pairs={{0,4},{4,0},{8,12},{12,8},{16,20},{20,16},{24,28},{28,24},{1,5},{5... | collective-permute-start | bytes 7077896 | tf_op jit(solution)/shard_map/ppermute | solution.py:529
  355.3 22.4 %collective-permute-start.45 = (bf16[3,192,384]{2,1,0:T(8,128)(2,1)S(1)}, bf16[3,192,384]{2,1,0:T(8,128)(2,1)S(1)}, u32[]{:S(2)}, u32[]{:S(2)}) collective-permute-start(bf16[3,192,384]{2,1,0:T(8,128)(2,1)S(1)} %get-tuple-element.125), channel_id=1, source_target_pairs={{0,16},{4,20},{8,24},{12,28},{16,0},{20,4},{24,8},{28,12},{1,17},{... | collective-permute-start | bytes 1327112 | tf_op jit(solution)/shard_map/ppermute | solution.py:535
  400.6 85.7 %collective-permute-start.42 = (bf16[512,768]{1,0:T(8,128)(2,1)S(1)}, bf16[512,768]{1,0:T(8,128)(2,1)S(1)}, u32[]{:S(2)}, u32[]{:S(2)}) collective-permute-start(bf16[512,768]{1,0:T(8,128)(2,1)S(1)} %get-tuple-element.129), channel_id=1, source_target_pairs={{0,0},{1,1},{4,2},{5,3},{2,4},{3,5},{6,6},{7,7},{8,8},{9,9},{12,10... | collective-permute-start | bytes 2359304 | tf_op jit(solution)/shard_map/ppermute | solution.py:557
  401.3 85.0 %collective-permute-start.43 = (bf16[512,768]{1,0:T(8,128)(2,1)S(1)}, bf16[512,768]{1,0:T(8,128)(2,1)S(1)}, u32[]{:S(2)}, u32[]{:S(2)}) collective-permute-start(bf16[512,768]{1,0:T(8,128)(2,1)S(1)} %get-tuple-element.130), channel_id=1, source_target_pairs={{1,0},{0,1},{5,2},{4,3},{3,4},{2,5},{7,6},{6,7},{9,8},{8,9},{13,10... | collective-permute-start | bytes 2359304 | tf_op jit(solution)/shard_map/ppermute | solution.py:557
  407.0 28.1 %collective-permute-start.77 = (bf16[96,3072]{1,0:T(8,128)(2,1)S(1)}, bf16[96,3072]{1,0:T(8,128)(2,1)S(1)}, u32[]{:S(2)}, u32[]{:S(2)}) collective-permute-start(bf16[96,3072]{1,0:T(8,128)(2,1)S(1)} %get-tuple-element.120), channel_id=1, source_target_pairs={{0,16},{4,20},{8,24},{12,28},{16,0},{20,4},{24,8},{28,12},{1,17},{... | collective-permute-start | bytes 1769480 | tf_op jit(solution)/shard_map/ppermute | solution.py:535
  407.8 27.2 %collective-permute-start.78 = (bf16[96,3072]{1,0:T(8,128)(2,1)S(1)}, bf16[96,3072]{1,0:T(8,128)(2,1)S(1)}, u32[]{:S(2)}, u32[]{:S(2)}) collective-permute-start(bf16[96,3072]{1,0:T(8,128)(2,1)S(1)} %get-tuple-element.119), channel_id=1, source_target_pairs={{0,24},{4,28},{8,16},{12,20},{16,8},{20,12},{24,0},{28,4},{1,25},{... | collective-permute-start | bytes 1769480 | tf_op jit(solution)/shard_map/ppermute | solution.py:535
  422.3 25.3 %collective-permute-start.69 = (bf16[96,3072]{1,0:T(8,128)(2,1)S(1)}, bf16[96,3072]{1,0:T(8,128)(2,1)S(1)}, u32[]{:S(2)}, u32[]{:S(2)}) collective-permute-start(bf16[96,3072]{1,0:T(8,128)(2,1)S(1)} %get-tuple-element.121), channel_id=1, source_target_pairs={{0,8},{4,12},{8,0},{12,4},{16,24},{20,28},{24,16},{28,20},{1,9},{5... | collective-permute-start | bytes 1769480 | tf_op jit(solution)/shard_map/ppermute | solution.py:535
  435.0 27.8 %collective-permute-start.70 = (bf16[96,3072]{1,0:T(8,128)(2,1)S(1)}, bf16[96,3072]{1,0:T(8,128)(2,1)S(1)}, u32[]{:S(2)}, u32[]{:S(2)}) collective-permute-start(bf16[96,3072]{1,0:T(8,128)(2,1)S(1)} %get-tuple-element.123), channel_id=1, source_target_pairs={{0,16},{4,20},{8,24},{12,28},{16,0},{20,4},{24,8},{28,12},{1,17},{... | collective-permute-start | bytes 1769480 | tf_op jit(solution)/shard_map/ppermute | solution.py:535
  435.0 27.8 %collective-permute-start.71 = (bf16[96,3072]{1,0:T(8,128)(2,1)S(1)}, bf16[96,3072]{1,0:T(8,128)(2,1)S(1)}, u32[]{:S(2)}, u32[]{:S(2)}) collective-permute-start(bf16[96,3072]{1,0:T(8,128)(2,1)S(1)} %get-tuple-element.122), channel_id=1, source_target_pairs={{0,24},{4,28},{8,16},{12,20},{16,8},{20,12},{24,0},{28,4},{1,25},{... | collective-permute-start | bytes 1769480 | tf_op jit(solution)/shard_map/ppermute | solution.py:535
  (89 other events, 1176.5 us)
where the time goes:
time: 490 us; the launch traced here: 488 us
  waiting for transfers between devices  159 us (32%)
  Pallas kernels  159 us (32%)
  starting transfers between devices  113 us (23%)
  other arithmetic  31.6 us (6%)
  local copies, waits for them, and re-layouts  23.2 us (5%)
    ppermute x21, waiting for transfers between devices, chip_step(): return lax.ppermute(x, 'dp', [(i, i ^ 2 * k) for i in range(ndp)])  99.4 us
    pallas_call x1, Pallas kernels, dense(): pl.pallas_call(functools.partial(dense_kernel, n_o=len(o_pieces), n_w=len...  54 us
    pallas_call x1, Pallas kernels, attend_back(): pl.pallas_call(functools.partial(attend_back_kernel, rows=rows, hs=hs, bl...  47.7 us
    ppermute x25, waiting for transfers between devices, z_step(): return lax.ppermute(x, 'tensor', [(i, i ^ k) for i in range(nt)])  39.4 us
    ppermute x25, starting transfers between devices, z_step(): return lax.ppermute(x, 'tensor', [(i, i ^ k) for i in range(nt)])  34 us
    pallas_call x3, Pallas kernels, weight_grad(): pl.pallas_call(functools.partial(grad_kernel, n_r=len(rights), drows=drow...  29.7 us
    pallas_call x1, Pallas kernels, attend(): pl.pallas_call(functools.partial(attend_kernel, rows=rows, hs=hs, blocks=...  27.5 us
    ppermute x21, starting transfers between devices, chip_step(): return lax.ppermute(x, 'dp', [(i, i ^ 2 * k) for i in range(ndp)])  24.9 us
  transfers between devices with their start and end apart: 82, of which 22 were waited for; matrix products, arithmetic and copies ran while one was open for 10% of the time, Pallas kernels for 22%

commit v1 on v0

v1 whole, which is shorter than its diff:
```python
import functools

import jax
import jax.numpy as jnp
from jax import lax
from jax.experimental import pallas as pl
from jax.experimental.pallas import tpu as pltpu
from jax.sharding import PartitionSpec as P

EPS = 1e-06
NEG = -1e30
BOTH = ("dp", "tensor")
F32 = jnp.float32
BF16 = jnp.bfloat16
ANY = pl.BlockSpec(memory_space=pl.ANY)
LIMIT = 58 << 20


def mm(left, right):
    return lax.dot_general(left, right, (((1,), (0,)), ((), ())), preferred_element_type=F32)


def mm_rt(left, right):
    return lax.dot_general(left, right, (((1,), (1,)), ((), ())), preferred_element_type=F32)


def mm_lt(left, right):
    return lax.dot_general(left, right, (((0,), (0,)), ((), ())), preferred_element_type=F32)


def head_lanes(shape, head, dim, head_size):
    place = lax.broadcasted_iota(jnp.int32, shape, dim)
    return (place < head_size) if head == 0 else (place >= head_size)


def fetches(pieces, offsets, target, dim, sems, first):
    copies = []
    for k, (piece, offset) in enumerate(zip(pieces, offsets)):
        count = piece.shape[dim]
        where = pl.ds(offset if isinstance(offset, int) else pl.multiple_of(offset, count), count)
        index = (slice(None),) * dim + (where,)
        copies.append(pltpu.make_async_copy(piece, target.at[index], sems.at[first + k]))
    return copies


def piece_rows(place, step, rows, count):
    if count == 1:
        return [0]
    return [(place ^ (k * step)) * rows for k in range(count)]


def attend_kernel(pair_ref, place_ref, *refs, rows, hs, blocks, n_w):
    x_refs, refs = refs[:2], refs[2:]
    w_refs, refs = refs[:n_w], refs[n_w:]
    bias_ref, segq_ref, segk_ref, q_out, k_out, v_out, o_mine, o_other, lse_ref, w_all, x_all, sems = refs
    group, block = pl.program_id(0), pl.program_id(1)
    lanes2 = 2 * hs

    @pl.when((group == 0) & (block == 0))
    def _():
        chip = place_ref[0] // 2
        w_parts = [piece.at[: w_all.shape[0]] for piece in w_refs]
        copies = fetches(
            w_parts, piece_rows(chip, 1, w_refs[0].shape[1], n_w), w_all, 1, sems, 0
        ) + fetches(x_refs, [0, x_refs[0].shape[0]], x_all, 0, sems, n_w)
        for copy in copies:
            copy.start()
        for copy in copies:
            copy.wait()

    @pl.when(block == 0)
    def _():
        weight = w_all[group]
        for k in range(blocks):
            part = pl.ds(k * rows, rows)
            out = (mm(x_all[part, :], weight) + bias_ref[0]).astype(BF16)
            q_out[part, :] = out[:, :lanes2] * (hs**-0.5)
            k_out[part, :] = out[:, lanes2 : 2 * lanes2]
            v_out[part, :] = out[:, 2 * lanes2 :]

    own = pl.ds(pl.multiple_of(block * rows, rows), rows)
    q2 = q_out[own, :]
    own_raw = (q2.astype(F32) * k_out[own, :].astype(F32)).T
    own_values = v_out[own, :].astype(F32).T
    segq = segq_ref[...]
    total = jnp.zeros((2 * hs, rows), F32)
    for head in range(2):
        target = pair_ref[2 * group + head, block]
        there = pl.ds(pl.multiple_of(target * rows, rows), rows)
        keys, values = k_out[there, :], v_out[there, :]
        lanes = head_lanes(q2.shape, head, 1, hs)
        scores = mm_rt(keys, jnp.where(lanes, q2, jnp.zeros_like(q2)))
        scores = jnp.where(segk_ref[there, :] == segq, scores, NEG)
        raw = jnp.sum(own_raw[head * hs : (head + 1) * hs], axis=0, keepdims=True)
        raw = jnp.where(target != block, raw, NEG)
        peak = jnp.maximum(jnp.max(scores, axis=0, keepdims=True), raw)
        expo = jnp.exp(scores - peak)
        own_expo = jnp.exp(raw - peak)
        denom = jnp.sum(expo, axis=0, keepdims=True) + own_expo
        masked_values = jnp.where(lanes, values, jnp.zeros_like(values))
        part = mm_lt(masked_values, expo.astype(BF16))
        low = own_expo.astype(BF16).astype(F32)
        mine = head_lanes(part.shape, head, 0, hs)
        part = part + jnp.where(mine, own_values * low, 0.0)
        total = total + part * (1.0 / denom)
        lse_ref[0, head : head + 1, :] = peak + jnp.log(denom)
    mixed = total.T.astype(BF16)

    @pl.when(block < blocks // 2)
    def _():
        o_mine[pl.ds(pl.multiple_of(block * rows, rows), rows), :] = mixed

    @pl.when(block >= blocks // 2)
    def _():
        o_other[pl.ds(pl.multiple_of((block - blocks // 2) * rows, rows), rows), :] = mixed


def attend(pairs, place, x_parts, w_pieces, bias, segq, segk, hs):
    heads, blocks = pairs.shape
    width = x_parts[0].shape[1]
    seq, groups, lanes = 2 * x_parts[0].shape[0], heads // 2, 2 * hs
    rows = seq // blocks
    kept = jax.ShapeDtypeStruct((seq, groups * lanes), BF16)
    flops = 2 * seq * width * 3 * groups * lanes + 4 * heads * seq * rows * 2 * lanes
    return pl.pallas_call(
        functools.partial(attend_kernel, rows=rows, hs=hs, blocks=blocks, n_w=len(w_pieces)),
        grid_spec=pltpu.PrefetchScalarGridSpec(
            num_scalar_prefetch=2,
            grid=(groups, blocks),
            in_specs=[ANY] * (2 + len(w_pieces))
            + [
                pl.BlockSpec((1, 1, 3 * lanes), lambda g, i, p, q: (g, 0, 0)),
                pl.BlockSpec((1, rows), lambda g, i, p, q: (0, i)),
                pl.BlockSpec((seq, 1), lambda g, i, p, q: (0, 0)),
            ],
            out_specs=[pl.BlockSpec((seq, lanes), lambda g, i, p, q: (0, g))] * 3
            + [
                pl.BlockSpec((seq // 2, lanes), lambda g, i, p, q: (0, g)),
                pl.BlockSpec((seq // 2, lanes), lambda g, i, p, q: (0, g)),
                pl.BlockSpec((1, 8, rows), lambda g, i, p, q: (g, 0, i)),
                pl.BlockSpec((groups, width, 3 * lanes), lambda g, i, p, q: (0, 0, 0)),
            ],
            scratch_shapes=[
                pltpu.VMEM((seq, width), BF16),
                pltpu.SemaphoreType.DMA((2 + len(w_pieces),)),
            ],
        ),
        out_shape=[kept] * 3
        + [jax.ShapeDtypeStruct((seq // 2, groups * lanes), BF16)] * 2
        + [
            jax.ShapeDtypeStruct((groups, 8, seq), F32),
            jax.ShapeDtypeStruct((groups, width, 3 * lanes), BF16),
        ],
        compiler_params=pltpu.CompilerParams(vmem_limit_bytes=LIMIT),
        cost_estimate=pl.CostEstimate(flops=flops, bytes_accessed=20 << 20, transcendentals=0),
        name="attend",
    )(pairs, place, *x_parts, *w_pieces, bias, segq, segk)


def attend_back_kernel(
    pair_ref, group_ref, q_ref, k_ref, v_ref, do_a, do_b, segq_ref, segk_ref, lse_ref,
    packed_ref, sums_ref, dq_all, dk_acc, dv_acc, *, rows, hs, blocks,
):
    block = pl.program_id(0)

    @pl.when(block == 0)
    def _():
        dk_acc[...] = jnp.zeros_like(dk_acc)
        dv_acc[...] = jnp.zeros_like(dv_acc)
        sums_ref[...] = jnp.zeros_like(sums_ref)

    own = pl.ds(pl.multiple_of(block * rows, rows), rows)
    q2, do2 = q_ref[...], jnp.where(block < blocks // 2, do_a[...], do_b[...])
    qt, dot = q2.astype(F32).T, do2.astype(F32).T
    own_keys, own_values = k_ref[own, :].astype(F32).T, v_ref[own, :].astype(F32).T
    own_raw, own_dp = qt * own_keys, dot * own_values
    segq = segq_ref[...]
    dq = jnp.zeros((2 * hs, rows), F32)
    own_ds, own_low = [], []
    for head in range(2):
        target = pair_ref[2 * group_ref[0] + head, block]
        there = pl.ds(pl.multiple_of(target * rows, rows), rows)
        keys, values = k_ref[there, :], v_ref[there, :]
        lanes = head_lanes(q2.shape, head, 1, hs)
        zero = jnp.zeros_like(q2)
        qm, dom = jnp.where(lanes, q2, zero), jnp.where(lanes, do2, zero)
        lse = lse_ref[0, head : head + 1, :]
        scores = mm_rt(keys, qm)
        probs = jnp.exp(jnp.where(segk_ref[there, :] == segq, scores - lse, NEG))
        raw = jnp.sum(own_raw[head * hs : (head + 1) * hs], axis=0, keepdims=True)
        self_prob = jnp.exp(jnp.where(target != block, raw - lse, NEG))
        self_dp = jnp.sum(own_dp[head * hs : (head + 1) * hs], axis=0, keepdims=True)
        dv_acc[there, :] += mm(probs.astype(BF16), dom)
        dprobs = mm_rt(values, dom)
        delta = jnp.sum(probs * dprobs, axis=0, keepdims=True) + self_prob * self_dp
        dscores = (probs * (dprobs - delta)).astype(BF16)
        dk_acc[there, :] += mm(dscores, qm)
        dq = dq + mm_lt(jnp.where(lanes, keys, jnp.zeros_like(keys)), dscores)
        own_ds.append((self_prob * (self_dp - delta)).astype(BF16).astype(F32))
        own_low.append(self_prob.astype(BF16).astype(F32))
    first = head_lanes(dq.shape, 0, 0, hs)
    ds_rows = jnp.where(first, own_ds[0], own_ds[1])
    low_rows = jnp.where(first, own_low[0], own_low[1])
    dq = ((dq + ds_rows * own_keys) * (hs**-0.5)).T
    dq_all[own, :] = dq.astype(BF16)
    sums_ref[0:1, :] += jnp.sum(dq, axis=0, keepdims=True)
    dk_acc[own, :] += (ds_rows * qt).T
    dv_acc[own, :] += (low_rows * dot).T

    @pl.when(block == blocks - 1)
    def _():
        dv = dv_acc[...]
        sums_ref[1:2, :] = jnp.sum(dv, axis=0, keepdims=True)
        packed_ref[...] = jnp.concatenate(
            [dq_all[...], dk_acc[...].astype(BF16), dv.astype(BF16)], axis=1
        )


def attend_back(pairs, group, q, k, v, grad_a, grad_b, segq, segk, lse, hs):
    heads, blocks = pairs.shape
    seq, lanes = q.shape[0], 2 * hs
    rows, half = seq // blocks, blocks // 2
    return pl.pallas_call(
        functools.partial(attend_back_kernel, rows=rows, hs=hs, blocks=blocks),
        grid_spec=pltpu.PrefetchScalarGridSpec(
            num_scalar_prefetch=2,
            grid=(blocks,),
            in_specs=[
                pl.BlockSpec((rows, lanes), lambda i, p, g: (i, g[0])),
                pl.BlockSpec((seq, lanes), lambda i, p, g: (0, g[0])),
                pl.BlockSpec((seq, lanes), lambda i, p, g: (0, g[0])),
                pl.BlockSpec((rows, lanes), lambda i, p, g: (jnp.minimum(i, half - 1), g[0])),
                pl.BlockSpec((rows, lanes), lambda i, p, g: (jnp.maximum(i - half, 0), g[0])),
                pl.BlockSpec((1, rows), lambda i, p, g: (0, i)),
                pl.BlockSpec((seq, 1), lambda i, p, g: (0, 0)),
                pl.BlockSpec((1, 8, rows), lambda i, p, g: (g[0], 0, i)),
            ],
            out_specs=[
                pl.BlockSpec((seq, 3 * lanes), lambda i, p, g: (0, 0)),
                pl.BlockSpec((8, lanes), lambda i, p, g: (0, 0)),
            ],
            scratch_shapes=[
                pltpu.VMEM((seq, lanes), BF16),
                pltpu.VMEM((seq, lanes), F32),
                pltpu.VMEM((seq, lanes), F32),
            ],
        ),
        out_shape=[
            jax.ShapeDtypeStruct((seq, 3 * lanes), BF16),
            jax.ShapeDtypeStruct((8, lanes), F32),
        ],
        compiler_params=pltpu.CompilerParams(vmem_limit_bytes=LIMIT),
        cost_estimate=pl.CostEstimate(
            flops=10 * 2 * seq * rows * 2 * lanes, bytes_accessed=6 << 20, transcendentals=0
        ),
        name="attend_back",
    )(pairs, jnp.full((1,), group, jnp.int32), q, k, v, grad_a, grad_b, segq, segk, lse)


def qkv_grad_kernel(place_ref, xa_ref, xb_ref, p0_ref, p1_ref, p2_ref, keep_ref, send_ref, acc):
    half = xa_ref.shape[0]
    chip = place_ref[0] // 2
    rows = keep_ref.shape[2]
    for j, packed in enumerate((p0_ref, p2_ref, p1_ref)):
        acc[...] = mm_lt(xa_ref[...], packed[:half, :]) + mm_lt(xb_ref[...], packed[half:, :])
        for k, away in enumerate(away_of(j == 2)):
            ours = acc[pl.ds(pl.multiple_of((chip ^ away) * rows, rows), rows), :]
            if k < 2:
                keep_ref[j, k] = ours
            else:
                send_ref[j, k - 2] = ours.astype(BF16)


def qkv_grads(place, x_parts, packed, rows):
    half, width = x_parts[0].shape
    cols = packed[0].shape[1]
    whole = lambda a, b: pl.BlockSpec((a, b), lambda i, p: (0, 0))
    part = pl.BlockSpec((3, 2, rows, cols), lambda i, p: (0, 0, 0, 0))
    return pl.pallas_call(
        qkv_grad_kernel,
        grid_spec=pltpu.PrefetchScalarGridSpec(
            num_scalar_prefetch=1,
            grid=(1,),
            in_specs=[whole(half, width)] * 2 + [whole(2 * half, cols)] * 3,
            out_specs=[part, part],
            scratch_shapes=[pltpu.VMEM((width, cols), F32)],
        ),
        out_shape=[
            jax.ShapeDtypeStruct((3, 2, rows, cols), F32),
            jax.ShapeDtypeStruct((3, 2, rows, cols), BF16),
        ],
        compiler_params=pltpu.CompilerParams(vmem_limit_bytes=LIMIT),
        cost_estimate=pl.CostEstimate(
            flops=12 * half * width * cols, bytes_accessed=12 << 20, transcendentals=0
        ),
        name="qkv_grads",
    )(place, *x_parts, *packed)


def in_grad_kernel(*refs, n, adds):
    packed, w_ref = refs[:n], refs[n]
    total = mm_rt(packed[0][...], w_ref[0])
    for g in range(1, n):
        total = total + mm_rt(packed[g][...], w_ref[g])
    for extra in refs[n + 1 : n + 1 + adds]:
        total = total + extra[...].astype(F32)
    outs = refs[n + 1 + adds :]
    if len(outs) == 1:
        outs[0][...] = total.astype(BF16)
        return
    for k, out in enumerate(outs):

        @pl.when(pl.program_id(0) == k)
        def _(out=out):
            out[...] = total.astype(BF16)


def in_grad(packed, weight, second, extras):
    seq, cols = packed[0].shape
    n, width = weight.shape[:2]
    tile = seq // 4
    first = 2 if second else 0
    return pl.pallas_call(
        functools.partial(in_grad_kernel, n=n, adds=len(extras)),
        grid=(2,),
        in_specs=[pl.BlockSpec((tile, cols), lambda i: (first + i, 0))] * n
        + [pl.BlockSpec((n, width, cols), lambda i: (0, 0, 0))]
        + [pl.BlockSpec((tile, width), lambda i: (i, 0))] * len(extras),
        out_specs=[pl.BlockSpec((tile, width), lambda i: (i, 0))]
        if second
        else [pl.BlockSpec((tile, width), lambda i: (0, 0))] * 2,
        out_shape=[jax.ShapeDtypeStruct((seq // 2, width), BF16)]
        if second
        else [jax.ShapeDtypeStruct((tile, width), BF16)] * 2,
        compiler_params=pltpu.CompilerParams(vmem_limit_bytes=LIMIT),
        cost_estimate=pl.CostEstimate(
            flops=seq * width * cols * n, bytes_accessed=8 << 20, transcendentals=0
        ),
        name="in_grad",
    )(*packed, weight, *extras)


def norm(values):
    centred = values - jnp.mean(values, axis=-1, keepdims=True)
    scale = lax.rsqrt(jnp.mean(centred * centred, axis=-1, keepdims=True) + EPS)
    return centred * scale, scale


def norm_back(grad, unit, scale, gain):
    q = grad * gain
    mean_q = jnp.mean(q, axis=-1, keepdims=True)
    mean_qn = jnp.mean(q * unit, axis=-1, keepdims=True)
    return scale * (q - mean_q - unit * mean_qn)


def gelu_parts(u):
    dense = jnp.exp(-0.5 * u * u) * 0.3989422804014327
    t = 1.0 / (1.0 + 0.2316419 * jnp.abs(u))
    poly = t * (
        0.319381530
        + t * (-0.356563782 + t * (1.781477937 + t * (-1.821255978 + t * 1.330274429)))
    )
    tail = dense * poly
    phi = jnp.where(u >= 0, 1.0 - tail, tail)
    return u * phi, phi + u * dense


def dense_copies(place, pieces, wo, ww, sems):
    copies = []

    def add(source, target):
        copies.append(pltpu.make_async_copy(source, target, sems.at[len(copies)]))

    if len(pieces) == 2:
        add(pieces[0], wo)
        add(pieces[1], ww)
        return copies
    core, chip = place % 2, place // 2
    chips, rows, cols = pieces[0].shape
    for side in range(2):
        lanes = pl.ds(pl.multiple_of((core ^ side) * cols, cols), cols)
        for k in range(chips):
            add(pieces[side].at[k], wo.at[pl.ds(pl.multiple_of((chip ^ k) * rows, rows), rows), lanes])
    half, rows = pieces[2].shape[1:3]
    for k, piece in enumerate(pieces[2:]):
        away = ((0, 1), (0, 2), (2, 3), (1, 3))[k % 4]
        for j in range(2):
            base = (place ^ (2 * away[j] + k // 4)) * rows
            add(piece.at[j], ww.at[pl.ds((k % 2) * half, half), pl.ds(pl.multiple_of(base, rows), rows), :])
    return copies


def dense_kernel(place_ref, *refs, n_w, chunks):
    w_refs, refs = refs[:n_w], refs[n_w:]
    (
        x_ref, mine_ref, other_ref, cot_a, cot_b, vec_ref, upb_ref,
        layer_a, layer_b, gm_mine, gm_other, act_ref, mlow_ref, gb_ref, gul_ref, ga_ref, gone_ref, sums_ref,
        wo, ww, slope, acc, sems,
    ) = refs
    step = pl.program_id(0)
    core = place_ref[0] % 2
    cols = mine_ref.shape[1]
    width = x_ref.shape[1]
    units = ww.shape[2] // 2

    @pl.when(step == 0)
    def _():
        copies = dense_copies(place_ref[0], w_refs, wo, ww, sems)
        for copy in copies:
            copy.start()
        for copy in copies:
            copy.wait()
        sums_ref[...] = jnp.zeros_like(sums_ref)

    mine_cols = pl.ds(pl.multiple_of(core * cols, cols), cols)
    other_cols = pl.ds(pl.multiple_of((1 - core) * cols, cols), cols)
    attn = mm_rt(mine_ref[...], wo[:, mine_cols]) + mm_rt(other_ref[...], wo[:, other_cols])
    unit_one, scale_one = norm(x_ref[...].astype(F32) + attn + vec_ref[0:1, :])
    middle = unit_one * vec_ref[1:2, :] + vec_ref[2:3, :]
    mlow_ref[...] = middle.astype(BF16)
    acc[...] = middle + vec_ref[3:4, :]

    @pl.loop(0, chunks)
    def _(k):
        place = pl.ds(pl.multiple_of(k * units, units), units)
        upper = mm(mlow_ref[...], ww[k, :, :units]) + upb_ref[:, place]
        active, rise = gelu_parts(upper)
        active = active.astype(BF16)
        act_ref[:, place] = active
        slope[:, place] = rise.astype(BF16)
        acc[...] += mm_rt(active, ww[k, :, units:])

    unit_two, scale_two = norm(acc[...])
    gain_two = vec_ref[4:5, :]
    layer = (unit_two * gain_two + vec_ref[5:6, :]).astype(BF16)

    @pl.when(step < pl.num_programs(0) // 2)
    def _():
        layer_a[...] = layer

    @pl.when(step >= pl.num_programs(0) // 2)
    def _():
        layer_b[...] = layer

    cot = jnp.where(step < pl.num_programs(0) // 2, cot_a[...], cot_b[...]).astype(F32)
    grad_two = norm_back(cot, unit_two, scale_two, gain_two)
    sums_ref[4:5, :] += jnp.sum(cot * unit_two, axis=0, keepdims=True)
    sums_ref[5:6, :] += jnp.sum(cot, axis=0, keepdims=True)
    sums_ref[3:4, :] += jnp.sum(grad_two, axis=0, keepdims=True)
    gb_ref[...] = grad_two.astype(BF16)
    acc[...] = grad_two

    @pl.loop(0, chunks)
    def _(k):
        place = pl.ds(pl.multiple_of(k * units, units), units)
        grad_upper = mm(gb_ref[...], ww[k, :, units:]) * slope[:, place].astype(F32)
        sums_ref[pl.ds(8 + (k ^ place_ref[1]), 1), :] += jnp.sum(grad_upper, axis=0, keepdims=True)
        grad_low = grad_upper.astype(BF16)
        gul_ref[:, place] = grad_low
        acc[...] += mm_rt(grad_low, ww[k, :, :units])

    grad_mid = acc[...]
    sums_ref[1:2, :] += jnp.sum(grad_mid * unit_one, axis=0, keepdims=True)
    sums_ref[2:3, :] += jnp.sum(grad_mid, axis=0, keepdims=True)
    grad_one = norm_back(grad_mid, unit_one, scale_one, vec_ref[1:2, :])
    sums_ref[0:1, :] += jnp.sum(grad_one, axis=0, keepdims=True)
    gone_ref[...] = grad_one
    grad_attn = grad_one.astype(BF16)
    ga_ref[...] = grad_attn
    gm_mine[...] = mm(grad_attn, wo[:, mine_cols]).astype(BF16)
    gm_other[...] = mm(grad_attn, wo[:, other_cols]).astype(BF16)


def dense(place, w_pieces, x, mine, other, cot_a, cot_b, vec, upb, tile):
    count, width = x.shape
    cols = other.shape[1]
    units = w_pieces[-1].shape[-1] // 2
    chunks = upb.shape[1] // units
    steps = count // tile
    half = steps // 2
    n_copies = 2 if len(w_pieces) == 2 else 2 * w_pieces[0].shape[0] + 2 * (len(w_pieces) - 2)
    rows = lambda n: pl.BlockSpec((tile, n), lambda i, p: (i, 0))
    fixed = lambda a, b: pl.BlockSpec((a, b), lambda i, p: (0, 0))
    full = chunks * units
    shapes = [
        ((count // 2, width), BF16), ((count // 2, width), BF16),
        ((count, cols), BF16), ((count, cols), BF16), ((count, full), BF16),
        ((count, width), BF16), ((count, width), BF16), ((count, full), BF16), ((count, width), BF16),
        ((count, width), F32), ((16, width), F32),
    ]
    flops = 8 * count * width * full + 4 * count * width * 2 * cols
    return pl.pallas_call(
        functools.partial(dense_kernel, n_w=len(w_pieces), chunks=chunks),
        grid_spec=pltpu.PrefetchScalarGridSpec(
            num_scalar_prefetch=1,
            grid=(count // tile,),
            in_specs=[ANY] * len(w_pieces)
            + [rows(width), rows(cols), rows(cols)]
            + [
                pl.BlockSpec((tile, width), lambda i, p: (jnp.minimum(i, half - 1), 0)),
                pl.BlockSpec((tile, width), lambda i, p: (jnp.maximum(i - half, 0), 0)),
                fixed(8, width),
                fixed(1, full),
            ],
            out_specs=[
                pl.BlockSpec((tile, width), lambda i, p: (jnp.minimum(i, half - 1), 0)),
                pl.BlockSpec((tile, width), lambda i, p: (jnp.maximum(i - half, 0), 0)),
                rows(cols), rows(cols), rows(full), rows(width), rows(width), rows(full),
                rows(width), rows(width), fixed(16, width),
            ],
            scratch_shapes=[
                pltpu.VMEM((width, 2 * cols), BF16),
                pltpu.VMEM((chunks, width, 2 * units), BF16),
                pltpu.VMEM((tile, full), BF16),
                pltpu.VMEM((tile, width), F32),
                pltpu.SemaphoreType.DMA((n_copies,)),
            ],
        ),
        out_shape=[jax.ShapeDtypeStruct(*s) for s in shapes],
        compiler_params=pltpu.CompilerParams(vmem_limit_bytes=LIMIT),
        cost_estimate=pl.CostEstimate(flops=flops, bytes_accessed=40 << 20, transcendentals=0),
        name="dense",
    )(place, *w_pieces, x, mine, other, cot_a, cot_b, vec, upb)


def away_of(second):
    return [0, jnp.where(second, 1, 2), jnp.where(second, 2, 1), 3]


def grad_kernel(place_ref, *refs, n, steps, drows, first):
    left_ref, right_ref, refs = refs[0], refs[1], refs[2:]
    extra, (keep_ref, send_ref, theirs_ref, left_t, acc) = refs[: n - 2], refs[n - 2 :]
    core, chip = place_ref[0] % 2, place_ref[0] // 2
    step = pl.program_id(0)

    @pl.when(step == 0)
    def _():
        left_t[...] = left_ref[...].T

    @pl.when(step >= steps)
    def _():
        acc[...] = mm(left_t[...], right_ref[...])

    if extra:

        @pl.when(step < steps)
        def _():
            cols = extra[1].shape[1]
            mine_cols = pl.ds(pl.multiple_of(core * cols, cols), cols)
            other_cols = pl.ds(pl.multiple_of((1 - core) * cols, cols), cols)
            acc[:, mine_cols] = mm_lt(extra[0][...], extra[1][...])
            acc[:, other_cols] = mm_lt(extra[0][...], extra[2][...])

    for k, away in enumerate(away_of(step >= first)):
        base = 2 * (chip ^ away)
        ours = acc[pl.ds(pl.multiple_of((base + core) * drows, drows), drows), :]
        if k < 2:
            keep_ref[0, k] = ours
        else:
            send_ref[0, k - 2] = ours.astype(BF16)
        theirs_ref[0, k] = acc[pl.ds(pl.multiple_of((base + 1 - core) * drows, drows), drows), :].astype(BF16)


def weight_grad(place, left, right, extra, drows, first):
    count, width = left.shape
    tile = width
    steps = 1 if extra else 0
    chunks = right.shape[1] // tile + steps
    whole = lambda a, b: pl.BlockSpec((a, b), lambda i, p: (0, 0))
    shapes = [((chunks, 2, drows, tile), F32), ((chunks, 2, drows, tile), BF16), ((chunks, 4, drows, tile), BF16)]
    return pl.pallas_call(
        functools.partial(grad_kernel, n=2 + len(extra), steps=steps, drows=drows, first=first),
        grid_spec=pltpu.PrefetchScalarGridSpec(
            num_scalar_prefetch=1,
            grid=(chunks,),
            in_specs=[
                whole(count, width),
                pl.BlockSpec((count, tile), lambda i, p: (0, jnp.maximum(i - steps, 0))),
            ]
            + [whole(count, e.shape[1]) for e in extra],
            out_specs=[pl.BlockSpec((1,) + shape[1:], lambda i, p: (i, 0, 0, 0)) for shape, _ in shapes],
            scratch_shapes=[pltpu.VMEM((width, count), BF16), pltpu.VMEM((width, tile), F32)],
        ),
        out_shape=[jax.ShapeDtypeStruct(*shape) for shape in shapes],
        compiler_params=pltpu.CompilerParams(vmem_limit_bytes=LIMIT),
        cost_estimate=pl.CostEstimate(
            flops=2 * count * width * chunks * tile, bytes_accessed=6 * chunks * width * tile, transcendentals=0
        ),
        name="weight_grad",
    )(place, left, right, *extra)


def xor_order(parts, index):
    parts = list(parts)
    bit = 1
    while bit < len(parts):
        odd = (index // bit) % 2 == 1
        parts = [jnp.where(odd, parts[k ^ bit], parts[k]) for k in range(len(parts))]
        bit *= 2
    return parts


def per_device(
    tokens,
    segments,
    pairing,
    qkv_weight,
    qv_bias,
    out_weight,
    out_bias,
    first_gain,
    first_shift,
    up_weight,
    up_bias,
    down_weight,
    down_bias,
    second_gain,
    second_shift,
    cotangent,
):
    width = tokens.shape[2]
    rows = tokens.shape[1]
    lheads, blocks = pairing.shape
    hs = qv_bias.shape[1] // 2
    lanes = 2 * hs
    units = up_weight.shape[1]
    ndp, nt = lax.axis_size("dp"), lax.axis_size("tensor")
    drows = width // ndp
    chips = ndp // 2
    dp, tensor = lax.axis_index("dp"), lax.axis_index("tensor")
    core, chip, half, low = dp % 2, dp // 2, tensor // 2, tensor % 2
    slot_mask = 2 * core + low
    heads = 2 * lheads
    cols = heads * hs
    aligned = drows % 8 == 0
    place = jnp.stack([dp, tensor]).astype(jnp.int32)
    order = [0, 1, 3, 4, 2, 5]

    core_pairs = [(i, i ^ 1) for i in range(ndp)]

    def core_swap(x):
        return lax.ppermute(x, "dp", core_pairs)

    def z_step(x, k):
        return lax.ppermute(x, "tensor", [(i, i ^ k) for i in range(nt)])

    def chip_step(x, k):
        return lax.ppermute(x, "dp", [(i, i ^ (2 * k)) for i in range(ndp)])

    def column(k, flip, back):
        steps = []
        for p in range(chips):
            for c in range(2):
                for a in range(2):
                    for b in range(2):
                        home = (2 * p + c) * nt + 2 * a + b
                        away = (2 * p + (a ^ flip)) * nt + 2 * c + (b ^ k)
                        steps.append((away, home) if back else (home, away))
        return steps

    def to_sequence(x):
        return [
            lax.ppermute(
                lax.dynamic_index_in_dim(x, low ^ k, 0, keepdims=False), BOTH, column(k, 0, False)
            )
            for k in range(2)
        ]

    def at_home(first, second):
        return jnp.stack([jnp.where(low == 0, first, second), jnp.where(low == 0, second, first)])

    def z_all(x):
        return [x] + [z_step(x, k) for k in range(1, nt)]

    def chip_all(x):
        return [x] + [chip_step(x, k) for k in range(1, chips)]

    gate = lambda *trees: lax.optimization_barrier(trees)

    qkv_local = qkv_weight.reshape(drows, lheads, 3, hs).transpose(0, 2, 1, 3)
    qkv_local = jnp.concatenate(
        [
            qkv_local[:, :, :2].reshape(drows, 3 * lanes),
            qkv_local[:, :, 2].reshape(drows, 3 * hs),
            out_weight.reshape(lheads * hs, drows).T,
        ],
        axis=1,
    )
    small = jnp.concatenate([pairing.astype(BF16).reshape(-1), qv_bias.reshape(-1), up_bias])
    n_pair, n_qv = lheads * blocks, lheads * lanes
    extra_rows = 8
    small = jnp.pad(small, (0, extra_rows * qkv_local.shape[1] - small.shape[0]))
    first_z = z_all(jnp.concatenate([qkv_local, small.reshape(extra_rows, -1)]))
    segs = jnp.where(half == core, segments, core_swap(segments))
    ff_local = jnp.concatenate([up_weight, down_weight.T], axis=1)
    ff_local, first_z = gate(ff_local, first_z)
    ff_one = z_step(ff_local, 1)

    abs_z = xor_order([part[:drows] for part in first_z], tensor)
    qkv_cols = 3 * lheads * hs

    def regroup(first, second):
        left, right = first[:, 3 * lanes : qkv_cols], second[:, 3 * lanes : qkv_cols]
        both = [part[:, hs * k : hs * (k + 1)] for k in range(3) for part in (left, right)]
        return jnp.stack([first[:, : 3 * lanes], second[:, : 3 * lanes], jnp.concatenate(both, axis=1)])

    def with_out(first, second):
        left, right = first[:, qkv_cols:], second[:, qkv_cols:]
        out = jnp.concatenate([left[:, :lanes], right[:, :lanes], left[:, lanes:], right[:, lanes:]], axis=1)
        return jnp.concatenate([regroup(first, second), out[None]])

    zero_heads, one_heads = with_out(abs_z[0], abs_z[1]), with_out(abs_z[2], abs_z[3])
    keep = jnp.where(core == 0, zero_heads, one_heads)
    got = core_swap(jnp.where(core == 0, one_heads, zero_heads))
    chip_rows = jnp.where(
        core == 0, jnp.concatenate([keep, got], axis=1), jnp.concatenate([got, keep], axis=1)
    )
    ff_pair = jnp.stack([ff_local, ff_one])
    chip_rows, ff_pair = gate(chip_rows, ff_pair)
    qkv_pieces = chip_all(chip_rows)
    ff_other = z_step(ff_pair, 2)

    tokens, ff_other = gate(tokens, ff_other)
    moved = to_sequence(tokens)
    qkv_pieces, ff_pair, ff_other = gate(qkv_pieces, ff_pair, ff_other)
    out_mine = jnp.stack([piece[3] for piece in qkv_pieces])
    if aligned:
        firsts = [chip_step(ff_pair, 1), chip_step(ff_other, 2)]
        out_other = core_swap(out_mine)
        x_mine = jnp.concatenate(moved)
        x_mine, firsts, out_other = gate(x_mine, firsts, out_other)
        twos = [jnp.stack([ff_pair, firsts[0]]), jnp.stack([ff_other, firsts[1]])]
        x_other = core_swap(x_mine)
        twos_swapped = [core_swap(two) for two in twos]
        fours = [chip_step(twos[0], 2), chip_step(twos[1], 1)]
        cotangent, x_mine, x_other, twos_swapped = gate(cotangent, x_mine, x_other, twos_swapped)
        cot_a, cot_b = to_sequence(cotangent)
    else:
        x_mine = jnp.concatenate(moved)
        x_other = core_swap(x_mine)
        cot_a, cot_b = to_sequence(cotangent)
        out_other = core_swap(out_mine)
        ff_own = chip_all(jnp.concatenate([ff_pair, ff_other]))
        ff_all = [part for piece in ff_own for part in (piece, core_swap(piece))]
        qkv_pieces = [jnp.concatenate(xor_order(qkv_pieces, chip), axis=1)]
        out_both = [jnp.concatenate(xor_order(list(o), chip)) for o in (out_mine, out_other)]
        dense_pieces = [
            jnp.concatenate(
                [jnp.where(core == 0, out_both[0], out_both[1]), jnp.where(core == 0, out_both[1], out_both[0])],
                axis=1,
            ),
            jnp.concatenate(xor_order(ff_all, dp), axis=1),
        ]

    small_rel = [part[drows:].reshape(-1) for part in first_z]
    small = jnp.stack(xor_order(small_rel, tensor))
    all_pairs = small[:, :n_pair].astype(jnp.int32).reshape(2, heads, blocks)
    my_pairs = jnp.where(core == 0, all_pairs[0], all_pairs[1])
    pair_slots = jnp.stack(xor_order([my_pairs[:, k] for k in range(blocks)], slot_mask), axis=1) ^ slot_mask
    pair_slots = jnp.stack([pair_slots[h] for h in order])
    all_qvb = small[:, n_pair : n_pair + n_qv].astype(F32).reshape(2, heads, lanes)
    my_qvb = jnp.where(core == 0, all_qvb[0], all_qvb[1])
    my_qvb = jnp.stack([my_qvb[h] for h in order])
    up_bias_rel = jnp.concatenate([s[n_pair + n_qv :][:units] for s in small_rel]).astype(F32)
    groups = heads // 2
    bias = jnp.concatenate(
        [
            my_qvb[:, :hs].reshape(groups, lanes),
            jnp.zeros((groups, lanes), F32),
            my_qvb[:, hs:].reshape(groups, lanes),
        ],
        axis=1,
    ).reshape(groups, 1, 3 * lanes)

    seg_rows = jnp.where(low == 0, segs[0], segs[1]).reshape(blocks, rows)
    seg_row = jnp.concatenate(xor_order([seg_rows[k] for k in range(blocks)], slot_mask))
    seg_col = seg_row.reshape(blocks * rows, 1)
    seg_row = seg_row.reshape(1, blocks * rows)

    x_parts = [x_mine, x_other]
    q, k, v, mixed, mixed_other, lse, w_all = attend(pair_slots, place, x_parts, qkv_pieces, bias, seg_row, seg_col, hs)
    if aligned:
        q, k, v, mixed, mixed_other, lse, w_all, fours, cot_a, cot_b = gate(
            q, k, v, mixed, mixed_other, lse, w_all, fours, cot_a, cot_b
        )
        dense_pieces = [out_mine, out_other] + twos + fours + twos_swapped + [core_swap(four) for four in fours]
    other = core_swap(mixed_other)

    blank = jnp.zeros((width,), BF16)
    vec = jnp.stack(
        [out_bias, first_gain, first_shift, down_bias, second_gain, second_shift, blank, blank]
    ).astype(F32)
    (
        layer_a, layer_b, gm_mine, gm_other, active, middle_low, grad_branch, grad_upper, grad_attn, grad_one, sums,
    ) = dense(
        place, dense_pieces, x_mine, mixed, other, cot_a, cot_b, vec, up_bias_rel.reshape(1, nt * units), 256
    )
    gm_got = core_swap(gm_other)
    home_0 = lax.ppermute(layer_a, BOTH, column(0, 0, True))

    def total_of(parts):
        total = parts[0].astype(F32)
        for part in parts[1:]:
            total = total + part.astype(F32)
        return total

    class Plane:
        def __init__(self, first, keep, send, got=None):
            self.first, self.got = first, got
            self.keep, self.send = self.split(keep), self.split(send)

        def split(self, x):
            return [x[: self.first], x[self.first :]]

        def first_sends(self):
            if self.got is None:
                return self.send
            got = self.split(self.got)
            self.keep = [[keep, g[:, :2]] for keep, g in zip(self.keep, got)]
            return [total_of([send, g[:, 2:]]).astype(BF16) for send, g in zip(self.send, got)]

        def first_moves(self, sends):
            return [chip_step(sends[0], 1), chip_step(sends[1], 2)]

        def second_sends(self, moves):
            keep = [k if isinstance(k, list) else [k] for k in self.keep]
            own = [total_of([part[:, 0] for part in k] + [m[:, 0]]) for k, m in zip(keep, moves)]
            sends = [total_of([part[:, 1] for part in k] + [m[:, 1]]).astype(BF16) for k, m in zip(keep, moves)]
            return own, sends

        def second_moves(self, sends):
            return [chip_step(sends[0], 2), chip_step(sends[1], 1)]

        def sums(self, own, moves):
            return [total_of([o, m]) for o, m in zip(own, moves)]

    class SlowPlane(Plane):
        def __init__(self, first, keep, send, got=None):
            self.first, self.view = first, keep if got is None else keep + got.astype(F32)

        def first_sends(self):
            return []

        def first_moves(self, sends):
            return []

        def second_sends(self, moves):
            return [], []

        def second_moves(self, sends):
            return []

        def sums(self, own, moves):
            pick = lambda step: lax.dynamic_index_in_dim(self.view, chip ^ step, 0, keepdims=False)
            total = total_of([pick(0)] + [chip_step(pick(step).astype(BF16), step) for step in range(1, chips)])
            return self.split(total.transpose(1, 0, 2))

    fast = chips == 4 and aligned

    def grads_of(left, right, extra, first):
        if fast:
            return weight_grad(place, left, right, extra, drows, first)
        grads = mm_lt(left, right)
        if extra:
            near, far = mm_lt(extra[0], extra[1]), mm_lt(extra[0], extra[2])
            head = [jnp.where(core == 0, near, far), jnp.where(core == 0, far, near)]
            grads = jnp.concatenate(head + [grads], axis=1)
        view = grads.reshape(chips, 2, drows, grads.shape[1] // width, width)
        ours = lax.dynamic_index_in_dim(view, core, 1, keepdims=False)
        theirs = lax.dynamic_index_in_dim(view, 1 - core, 1, keepdims=False).astype(BF16)
        return ours, theirs, theirs

    plane_of = Plane if fast else SlowPlane
    down_keep, down_send, down_theirs = grads_of(grad_branch, active, [], 2)
    down_got = core_swap(down_theirs)
    middle_low, down_keep, down_send, down_theirs, gm_got = gate(
        middle_low, down_keep, down_send, down_theirs, gm_got
    )
    up_keep, up_send, up_theirs = grads_of(middle_low, grad_upper, [grad_attn, mixed, other], 3)
    up_got = core_swap(up_theirs)

    down = plane_of(2, down_keep, down_send, down_got)
    d_sends = down.first_sends()
    pairs_0, gm_got, d_sends = gate(pair_slots, gm_got, d_sends)
    d_moves = down.first_moves(d_sends)
    packed_0, sums_0 = attend_back(pairs_0, 0, q, k, v, gm_mine, gm_got, seg_row, seg_col, lse, hs)
    packed_0, sums_0, d_moves, up_got, home_0 = gate(packed_0, sums_0, d_moves, up_got, home_0)
    d_own, d_sends = down.second_sends(d_moves)
    up = plane_of(3, up_keep, up_send, up_got)
    u_sends = up.first_sends()
    pairs_1, d_own, d_sends, u_sends = gate(pair_slots, d_own, d_sends, u_sends)
    d_moves = down.second_moves(d_sends)
    u_moves = up.first_moves(u_sends)
    packed_1, sums_1 = attend_back(pairs_1, 1, q, k, v, gm_mine, gm_got, seg_row, seg_col, lse, hs)
    packed_1, sums_1, d_moves, u_moves, layer_b = gate(packed_1, sums_1, d_moves, u_moves, layer_b)
    home_1 = lax.ppermute(layer_b, BOTH, column(1, 0, True))
    d_first, d_second = down.sums(d_own, d_moves)
    u_own, u_sends = up.second_sends(u_moves)
    d_second = d_second.astype(BF16)
    pair_slots, packed_1, d_first, d_second, u_own, u_sends = gate(
        pair_slots, packed_1, d_first, d_second, u_own, u_sends
    )
    d_second = z_step(d_second, 2)
    u_moves = up.second_moves(u_sends)
    packed_2, sums_2 = attend_back(pair_slots, 2, q, k, v, gm_mine, gm_got, seg_row, seg_col, lse, hs)
    packed_2, sums_2, u_moves, d_second = gate(packed_2, sums_2, u_moves, d_second)
    d_keep = total_of([d_first[0], d_second[0]])
    d_give = total_of([d_first[1], d_second[1]]).astype(BF16)
    u_first, u_second = up.sums(u_own, u_moves)
    out_near = jnp.where(half == 0, u_first[0, :, :cols], u_first[0, :, cols:])
    out_far = jnp.where(half == 0, u_first[0, :, cols:], u_first[0, :, :cols])
    u_first = u_first[1:]
    u_second, out_far = u_second.astype(BF16), out_far.astype(BF16)
    out_far = jnp.pad(out_far, ((0, 0), (0, width - cols)))
    u_second = jnp.concatenate([u_second, out_far[None]])

    head_sums = jnp.concatenate([part[row] for row in range(2) for part in (sums_0, sums_1, sums_2)])[None]
    blank = jnp.zeros_like(head_sums)
    sums = jnp.concatenate(
        [
            sums[:12],
            jnp.where(core == 0, head_sums, blank),
            jnp.where(core == 0, blank, head_sums),
            jnp.zeros((2, width), F32),
        ]
    )
    packed_2, d_keep, d_give, u_first, u_second, sums, out_near = gate(
        packed_2, d_keep, d_give, u_first, u_second, sums, out_near
    )
    packed = [packed_0, packed_1, packed_2]
    d_give = z_step(d_give, 1)
    u_second = z_step(u_second, 2)
    sums_got = z_step(sums, 1)
    (in_other,) = in_grad(packed, w_all, True, [])
    in_other, d_give, u_second, sums_got, packed_0, home_1 = gate(
        in_other, d_give, u_second, sums_got, packed_0, home_1
    )
    layer_out = at_home(home_0, home_1)
    down_grad = (d_keep + d_give.astype(F32)).T
    sums = sums + sums_got
    u_keep, u_give = [total_of([u_first[j], u_second[j]]) for j in range(2)]
    out_near = total_of([out_near, u_second[2, :, :cols]])

    def out_unit(wanted_low):
        parts = [
            jnp.concatenate(
                [out_near[:, lanes * w : lanes * (w + 1)], out_near[:, 2 * lanes + hs * w : 2 * lanes + hs * (w + 1)]],
                axis=1,
            )
            for w in range(2)
        ]
        return jnp.where(wanted_low == 0, parts[0], parts[1])

    u_give = jnp.concatenate([u_give, out_unit(1 - low)], axis=1).astype(BF16)
    out_near = out_unit(low)
    in_other, u_keep, u_give, sums, packed_0 = gate(in_other, u_keep, u_give, sums, packed_0)
    in_got = core_swap(in_other)
    u_give = z_step(u_give, 1)
    sums_got = z_step(sums, 2)
    if fast:
        qkv_keep, qkv_send = qkv_grads(place, x_parts, packed, 2 * drows)
    else:
        parts = [mm_lt(jnp.concatenate(x_parts), packed[g]).reshape(chips, 2 * drows, 3 * lanes) for g in (0, 2, 1)]
        qkv_keep = qkv_send = jnp.stack(parts, axis=2)
    qkv_keep, qkv_send, in_got, u_give, sums_got = gate(qkv_keep, qkv_send, in_got, u_give, sums_got)
    sums = sums + sums_got
    qkv = plane_of(2, qkv_keep, qkv_send)
    a_sends = qkv.first_sends()
    in_got, a_sends, sums = gate(in_got, a_sends, sums)
    a_moves = qkv.first_moves(a_sends)
    sums_got = core_swap(sums)
    in_low = in_grad(packed, w_all, False, [in_got, grad_one])
    in_low, a_moves, sums_got = gate(in_low, a_moves, sums_got)
    homes = [lax.ppermute(in_low[k], BOTH, column(k, 0, True)) for k in range(2)]
    a_own, a_sends = qkv.second_sends(a_moves)
    a_moves = qkv.second_moves(a_sends)
    sums = sums + sums_got
    up_grad = total_of([u_keep, u_give[:, :units]])
    out_grad = total_of([out_near, u_give[:, units:]]).T.reshape(lheads, hs, drows)
    for bit in range(chips.bit_length() - 1):
        sums = sums + chip_step(sums, 1 << bit)
    outb_grad, gain_one_grad, shift_one_grad, downb_grad, gain_two_grad, shift_two_grad = [
        sums[row] for row in range(6)
    ]
    upb_grad = lax.dynamic_index_in_dim(sums, 8 + tensor, 0, keepdims=False)
    head_row = jnp.where(half == 0, sums[12], sums[13]).reshape(2, 6, hs)
    qvb_grad = jnp.where(low == 0, head_row[:, [0, 1, 4]], head_row[:, [2, 3, 5]])
    qvb_grad = jnp.concatenate([qvb_grad[0], qvb_grad[1]], axis=1)

    homes, a_moves = gate(homes, a_moves)
    input_grad = at_home(*homes)
    sum_a, sum_b = qkv.sums(a_own, a_moves)
    sum_0, sum_2, sum_1 = [part.reshape(2, drows, 3 * lanes) for part in (sum_a[0], sum_a[1], sum_b[0])]
    sum_01 = [sum_0, sum_1]

    def share(c, u):
        third = [sum_2[c][:, lanes * k + hs * u : lanes * k + hs * (u + 1)] for k in range(3)]
        return jnp.concatenate([sum_01[u][c]] + third, axis=1)

    shares = [[share(c, u).astype(BF16) for u in range(2)] for c in range(2)]
    qkv_grad = jnp.zeros((drows, 3 * lheads * hs), F32)
    for flip in range(2):
        for step in range(2):
            by_core = [jnp.where((low ^ step) == 0, shares[c][0], shares[c][1]) for c in range(2)]
            sent = jnp.where((half ^ flip) == 0, by_core[0], by_core[1])
            qkv_grad = qkv_grad + lax.ppermute(sent, BOTH, column(step, flip, False)).astype(F32)
    pairs_part = qkv_grad[:, : 3 * lanes].reshape(drows, 3, 2, hs)
    third_part = qkv_grad[:, 3 * lanes :].reshape(drows, 3, 1, hs)
    qkv_grad = jnp.concatenate([pairs_part, third_part], axis=2).transpose(0, 2, 1, 3)
    qkv_grad = qkv_grad.reshape(drows, lheads, 3 * hs)
    return (
        layer_out,
        input_grad,
        qkv_grad,
        qvb_grad,
        out_grad,
        outb_grad,
        gain_one_grad,
        shift_one_grad,
        up_grad,
        upb_grad,
        down_grad,
        downb_grad,
        gain_two_grad,
        shift_two_grad,
    )


def solution(mesh):
    return jax.shard_map(
        per_device,
        mesh=mesh,
        in_specs=(
            P("dp", "tensor", None),
            P("dp", None),
            P("tensor", None),
            P("dp", "tensor", None),
            P("tensor", None),
            P("tensor", None, "dp"),
            P(),
            P(),
            P(),
            P("dp", "tensor"),
            P("tensor"),
            P("tensor", "dp"),
            P(),
            P(),
            P(),
            P("dp", "tensor", None),
        ),
        out_specs=(
            P("dp", "tensor", None),
            P("dp", "tensor", None),
            P("dp", "tensor", None),
            P("tensor", None),
            P("tensor", None, "dp"),
            P(),
            P(),
            P(),
            P("dp", "tensor"),
            P("tensor"),
            P("tensor", "dp"),
            P(),
            P(),
            P(),
        ),
        check_vma=False,
    )
```

time: 490 us -> 455 us (0.929)
  waiting for transfers between devices: 159 us -> 96.6 us
  Pallas kernels: 159 us -> 174 us
  other arithmetic: 31.6 us -> 39.8 us
    ppermute x21, waiting for transfers between devices: 99.4 us -> 15.4 us  [chip_step(): return lax.ppermute(x, 'dp', [(i, i ^ 2 * k) for i in range(ndp)])]
    pallas_call x4 -> x6, Pallas kernels: 83.7 us -> 104 us  [the longest x1 54.6 us: dense(): pl.pallas_call(functools.partial(dense_kernel, n_w=len(w_pieces), chunks=...]
    ppermute x4, starting transfers between devices: 6.79 us -> 21.8 us  [per_device(): lax.ppermute(sent, BOTH, column(step, flip, False)).astype(F32)]
    ppermute x4, waiting for transfers between devices: 0.01 us -> 12.9 us  [to_sequence(): lax.ppermute(lax.dynamic_index_in_dim(x, low ^ k, 0, keepdims=False), BOT...]
    convert_element_type x4 -> x14, other arithmetic: 4.98 us -> 17.3 us  [the longest x6 9.28 us: second_sends(): total_of([part[:, 1] for part in k] + [m[:, 1]]).astype(BF16)]
    ppermute x10 -> x4, waiting for transfers between devices: 16.6 us -> 5.86 us  [the longest x2 5.85 us: per_device(): lax.ppermute(in_low[k], BOTH, column(k, 0, True))]
    ppermute x4, starting transfers between devices: 13.2 us -> 2.58 us  [to_sequence(): lax.ppermute(lax.dynamic_index_in_dim(x, low ^ k, 0, keepdims=False), BOT...]
    ppermute x25 -> x11, waiting for transfers between devices: 39.4 us -> 49.7 us  [z_step(): return lax.ppermute(x, 'tensor', [(i, i ^ k) for i in range(nt)])]
  transfers between devices with their start and end apart: 82 -> 58, of which waited for: 22 -> 16; matrix products, arithmetic and copies ran while one was open for 10% -> 7% of each run, Pallas kernels for 22% -> 27%
where the time goes in v1:
time: 455 us; the launch traced here: 450 us
  Pallas kernels  174 us (38%)
  starting transfers between devices  111 us (24%)
  waiting for transfers between devices  96.6 us (21%)
  other arithmetic  39.8 us (9%)
  local copies, waits for them, and re-layouts  26.1 us (6%)
    pallas_call x1, Pallas kernels, dense(): pl.pallas_call(functools.partial(dense_kernel, n_w=len(w_pieces), chunks=...  54.6 us
    ppermute x11, waiting for transfers between devices, z_step(): return lax.ppermute(x, 'tensor', [(i, i ^ k) for i in range(nt)])  49.7 us
    pallas_call x3, Pallas kernels, attend_back(): pl.pallas_call(functools.partial(attend_back_kernel, rows=rows, hs=hs, bl...  40.5 us
    ppermute x11, starting transfers between devices, z_step(): return lax.ppermute(x, 'tensor', [(i, i ^ k) for i in range(nt)])  35.1 us
    pallas_call x1, Pallas kernels, attend(): pl.pallas_call(functools.partial(attend_kernel, rows=rows, hs=hs, blocks=...  29.7 us
    pallas_call x2, Pallas kernels, weight_grad(): pl.pallas_call(functools.partial(grad_kernel, n=2 + len(extra), steps=ste...  25.1 us
    ppermute x21, starting transfers between devices, chip_step(): return lax.ppermute(x, 'dp', [(i, i ^ 2 * k) for i in range(ndp)])  23.5 us
    ppermute x14, starting transfers between devices, core_swap(): return lax.ppermute(x, 'dp', core_pairs)  22.8 us
  transfers between devices with their start and end apart: 58, of which 16 were waited for; matrix products, arithmetic and copies ran while one was open for 7% of the time, Pallas kernels for 27%

profile of v1, /device:TPU:0, one launch (start us, length us, event | category | flops | bytes accessed | tf_op | source)
XLA Modules:
  0.0 449.5 jit_solution(8513974521915343794)
XLA Ops:
  5.3 3.1 collective-permute-start
  8.4 2.6 collective-permute-start.1
  14.9 8.3 %collective-permute-done.1 = bf16[104,768]{1,0:T(8,128)(2,1)S(1)} collective-permute-done((bf16[104,768]{1,0:T(8,128)(2,1)S(1)}, bf16[104,768]{1,0:T(8,128)(2,1)S(1)}, u32[]{:S(2)}, u32[]{:S(2)}) %collective-permute-start.1) | collective-permute-done | bytes 159776 | tf_op jit(solution)/shard_map/ppermute | solution.py:645
  29.7 3.2 collective-permute-done.4
  36.6 3.0 collective-permute-start.8
  43.4 20.4 %collective-permute-done.8 = bf16[2,96,1536]{2,1,0:T(8,128)(2,1)} collective-permute-done((bf16[2,96,1536]{2,1,0:T(8,128)(2,1)S(1)}, bf16[2,96,1536]{2,1,0:T(8,128)(2,1)}, u32[]{:S(2)}, u32[]{:S(2)}) %collective-permute-start.8) | collective-permute-done | bytes 589856 | tf_op jit(solution)/shard_map/ppermute | solution.py:645
  67.1 3.0 collective-permute-start.13
  74.0 12.9 %collective-permute-done.10 = bf16[512,768]{1,0:T(8,128)(2,1)S(1)} collective-permute-done((bf16[512,768]{1,0:T(8,128)(2,1)}, bf16[512,768]{1,0:T(8,128)(2,1)S(1)}, u32[]{:S(2)}, u32[]{:S(2)}) %collective-permute-start.10) | collective-permute-done | bytes 786464 | tf_op jit(solution)/shard_map/ppermute | solution.py:663
  88.1 13.5 %collective-permute-start.14 = (bf16[1024,768]{1,0:T(8,128)(2,1)}, bf16[1024,768]{1,0:T(8,128)(2,1)}, u32[]{:S(2)}, u32[]{:S(2)}) collective-permute-start(bf16[1024,768]{1,0:T(8,128)(2,1)} %pad_maximum_fusion.refs_0_.refs_10_.xa_ref), channel_id=1, source_target_pairs={{0,4},{4,0},{8,12},{12,8},{16,20},{20,16},{24,28},{28,24},{1,5},{5... | collective-permute-start | bytes 4718600 | tf_op jit(solution)/shard_map/ppermute | solution.py:642
  110.0 29.7 %attend.1 = (bf16[2048,384]{1,0:T(8,128)(2,1)}, bf16[2048,384]{1,0:T(8,128)(2,1)}, bf16[2048,384]{1,0:T(8,128)(2,1)}, bf16[1024,384]{1,0:T(8,128)(2,1)}, bf16[10...) custom-call(s32[6,4]{1,0:T(8,128)} %pad_add_fusion.1.pair_ref, s32[2]{0:T(128)} %pad_add_fusion.2.place_ref, ...), custom_call_target="tpu_custom_call" | custom-call | flops 10066329600 | bytes 20971520 | tf_op jit(solution)/shard_map/attend/pallas_call | solution.py:125
  140.6 3.9 collective-permute-start.22
  146.9 3.1 collective-permute-done.24.refs_12_.refs_4_
  152.3 54.6 %dense.1 = (bf16[512,768]{1,0:T(8,128)(2,1)}, bf16[512,768]{1,0:T(8,128)(2,1)}, bf16[1024,384]{1,0:T(8,128)(2,1)}, bf16[1024,384]{1,0:T(8,128)(2,1)}, bf16[1024,...) custom-call(s32[2]{0:T(128)} %pad_add_fusion.2.place_ref, ...), custom_call_target="tpu_custom_call" | custom-call | flops 21743271936 | bytes 41943040 | tf_op jit(solution)/shard_map/dense/pallas_call | solution.py:492
  207.4 10.8 %weight_grad.2 = (f32[4,2,96,768]{3,2,1,0:T(8,128)}, bf16[4,2,96,768]{3,2,1,0:T(8,128)(2,1)}, bf16[4,4,96,768]{3,2,1,0:T(8,128)(2,1)}) custom-call(s32[2]{0:T(128)} %pad_add_fusion.2.place_ref, bf16[1024,768]{1,0:T(8,128)(2,1)} %get-tuple-element.196.refs_0_, bf16[1024,3072]{1,0:T(8,128)(2,1)} %get-tuple-element.197.refs_1_), custom_call_target="tpu_custom_call" | custom-call | flops 4831838208 | bytes 14155776 | tf_op jit(solution)/shard_map/weight_grad/pallas_call | solution.py:571
  218.4 14.2 %weight_grad.3 = (f32[5,2,96,768]{3,2,1,0:T(8,128)}, bf16[5,2,96,768]{3,2,1,0:T(8,128)(2,1)}, bf16[5,4,96,768]{3,2,1,0:T(8,128)(2,1)}) custom-call(s32[2]{0:T(128)} %pad_add_fusion.2.place_ref, bf16[1024,768]{1,0:T(8,128)(2,1)} %get-tuple-element.215.refs_0_, bf16[1024,3072]{1,0:T(8,128)(2,1)} %get-tuple-element.216.refs_1_, ...), custom_call_target="tpu_custom_call" | custom-call | flops 6039797760 | bytes 17694720 | tf_op jit(solution)/shard_map/weight_grad/pallas_call | solution.py:571
  238.9 13.5 %attend_back.3 = (bf16[2048,384]{1,0:T(8,128)(2,1)}, f32[8,128]{1,0:T(8,128)}) custom-call(s32[6,4]{1,0:T(8,128)} %pad_add_fusion.1.pair_ref, s32[1]{0:T(128)} %constant.127.clone.1.group_ref, bf16[2048,384]{1,0:T(8,128)(2,1)} %get-tuple-element.205.q_ref, bf16[2048,384]{1,0:T(8,128)(2,1)} %get-tuple-element.206.k_ref, ...), custom_call_target="tpu_custom_call" | custom-call | flops 5368709120 | bytes 6291456 | tf_op jit(solution)/shard_map/attend_back/pallas_call | solution.py:223
  252.5 2.7 add_convert_fusion.1
  265.2 13.5 %attend_back.4 = (bf16[2048,384]{1,0:T(8,128)(2,1)}, f32[8,128]{1,0:T(8,128)}) custom-call(s32[6,4]{1,0:T(8,128)} %pad_add_fusion.1.pair_ref, s32[1]{0:T(128)} %constant.128.clone.1.group_ref, bf16[2048,384]{1,0:T(8,128)(2,1)} %get-tuple-element.205.q_ref, bf16[2048,384]{1,0:T(8,128)(2,1)} %get-tuple-element.206.k_ref, ...), custom_call_target="tpu_custom_call" | custom-call | flops 5368709120 | bytes 6291456 | tf_op jit(solution)/shard_map/attend_back/pallas_call | solution.py:223
  279.4 5.1 %collective-permute-done.32 = bf16[2,96,768]{2,1,0:T(8,128)(2,1)} collective-permute-done((bf16[2,96,768]{2,1,0:T(8,128)(2,1)}, bf16[2,96,768]{2,1,0:T(8,128)(2,1)}, u32[]{:S(2)}, u32[]{:S(2)}) %collective-permute-start.32) | collective-permute-done | bytes 294944 | tf_op jit(solution)/shard_map/ppermute | solution.py:648
  292.4 11.1 %collective-permute-start.37 = (bf16[2,96,768]{2,1,0:T(8,128)(2,1)S(1)}, bf16[2,96,768]{2,1,0:T(8,128)(2,1)S(1)}, u32[]{:S(2)}, u32[]{:S(2)}) collective-permute-start(bf16[2,96,768]{2,1,0:T(8,128)(2,1)S(1)} %add_convert_fusion.5), channel_id=1, source_target_pairs={{0,2},{1,3},{2,0},{3,1},{4,6},{5,7},{6,4},{7,5},{8,10},{9,11},{10,... | collective-permute-start | bytes 884744 | tf_op jit(solution)/shard_map/ppermute | solution.py:645
  304.0 13.5 %attend_back.5 = (bf16[2048,384]{1,0:T(8,128)(2,1)}, f32[8,128]{1,0:T(8,128)}) custom-call(s32[6,4]{1,0:T(8,128)} %pad_add_fusion.1.pair_ref, s32[1]{0:T(128)} %constant.129.clone.1.group_ref, bf16[2048,384]{1,0:T(8,128)(2,1)} %get-tuple-element.205.q_ref, bf16[2048,384]{1,0:T(8,128)(2,1)} %get-tuple-element.206.k_ref, ...), custom_call_target="tpu_custom_call" | custom-call | flops 5368709120 | bytes 6291456 | tf_op jit(solution)/shard_map/attend_back/pallas_call | solution.py:223
  322.2 9.1 %collective-permute-start.38 = (bf16[96,768]{1,0:T(8,128)(2,1)S(1)}, bf16[96,768]{1,0:T(8,128)(2,1)S(1)}, u32[]{:S(2)}, u32[]{:S(2)}) collective-permute-start(bf16[96,768]{1,0:T(8,128)(2,1)S(1)} %get-tuple-element.263), channel_id=1, source_target_pairs={{0,1},{1,0},{2,3},{3,2},{4,5},{5,4},{6,7},{7,6},{8,9},{9,8},{10,11... | collective-permute-start | bytes 442376 | tf_op jit(solution)/shard_map/ppermute | solution.py:645
  331.3 5.9 %in_grad.2 = bf16[1024,768]{1,0:T(8,128)(2,1)} custom-call(bf16[2048,384]{1,0:T(8,128)(2,1)} %get-tuple-element.221.refs_0_.p0_ref, bf16[2048,384]{1,0:T(8,128)(2,1)} %get-tuple-element.243.refs_1_.p1_ref, bf16[2048,384]{1,0:T(8,128)(2,1)} %get-tuple-element.261.refs_2_.p2_ref, bf16[3,768,384]{2,1,0:T(8,128)(2,1)} %get-tuple-element.262.refs_3_), custom_call_target="tpu_custom_call" | custom-call | flops 1811939328 | bytes 8388608 | tf_op jit(solution)/shard_map/in_grad/pallas_call | solution.py:323
  338.9 12.3 %collective-permute-done.39 = bf16[3,96,768]{2,1,0:T(8,128)(2,1)S(1)} collective-permute-done((bf16[3,96,768]{2,1,0:T(8,128)(2,1)S(1)}, bf16[3,96,768]{2,1,0:T(8,128)(2,1)S(1)}, u32[]{:S(2)}, u32[]{:S(2)}) %collective-permute-start.39) | collective-permute-done | bytes 442400 | tf_op jit(solution)/shard_map/ppermute | solution.py:645
  352.9 10.8 %qkv_grads.1 = (f32[3,2,192,384]{3,2,1,0:T(8,128)}, bf16[3,2,192,384]{3,2,1,0:T(8,128)(2,1)}) custom-call(s32[2]{0:T(128)} %pad_add_fusion.2.place_ref, bf16[1024,768]{1,0:T(8,128)(2,1)} %pad_maximum_fusion.refs_0_.refs_10_.xa_ref, bf16[1024,768]{1,0:T(8,128)(2,1)} %collective-permute-done.14.refs_1_.xb_ref, ...), custom_call_target="tpu_custom_call" | custom-call | flops 3623878656 | bytes 12582912 | tf_op jit(solution)/shard_map/qkv_grads/pallas_call | solution.py:279
  364.1 3.1 collective-permute-start.44
  376.5 7.4 %in_grad.3 = (bf16[512,768]{1,0:T(8,128)(2,1)}, bf16[512,768]{1,0:T(8,128)(2,1)}) custom-call(bf16[2048,384]{1,0:T(8,128)(2,1)} %get-tuple-element.221.refs_0_.p0_ref, bf16[2048,384]{1,0:T(8,128)(2,1)} %get-tuple-element.243.refs_1_.p1_ref, bf16[2048,384]{1,0:T(8,128)(2,1)} %get-tuple-element.261.refs_2_.p2_ref, ...), custom_call_target="tpu_custom_call" | custom-call | flops 1811939328 | bytes 8388608 | tf_op jit(solution)/shard_map/in_grad/pallas_call | solution.py:323
  384.6 4.4 collective-permute-done.45
  401.4 5.5 %collective-permute-done.50 = bf16[2,192,384]{2,1,0:T(8,128)(2,1)} collective-permute-done((bf16[2,192,384]{2,1,0:T(8,128)(2,1)}, bf16[2,192,384]{2,1,0:T(8,128)(2,1)}, u32[]{:S(2)}, u32[]{:S(2)}) %collective-permute-start.50) | collective-permute-done | bytes 294944 | tf_op jit(solution)/shard_map/ppermute | solution.py:648
  406.9 5.8 %collective-permute-done.49 = bf16[512,768]{1,0:T(8,128)(2,1)S(1)} collective-permute-done((bf16[512,768]{1,0:T(8,128)(2,1)}, bf16[512,768]{1,0:T(8,128)(2,1)S(1)}, u32[]{:S(2)}, u32[]{:S(2)}) %collective-permute-start.49) | collective-permute-done | bytes 786464 | tf_op jit(solution)/shard_map/ppermute | solution.py:974
  418.8 18.7 %collective-permute-start.54 = (bf16[96,576]{1,0:T(8,128)(2,1)S(1)}, bf16[96,576]{1,0:T(8,128)(2,1)S(1)}, u32[]{:S(2)}, u32[]{:S(2)}) collective-permute-start(bf16[96,576]{1,0:T(8,128)(2,1)S(1)} %broadcast_select_fusion.11), channel_id=1, source_target_pairs={{0,4},{1,5},{2,0},{3,1},{4,6},{5,7},{6,2},{7,3},{8,12},{9,13},{10,... | collective-permute-start | bytes 331784 | tf_op jit(solution)/shard_map/ppermute | solution.py:1006
  438.9 8.9 %collective-permute-done.54 = bf16[96,576]{1,0:T(8,128)(2,1)S(1)} collective-permute-done((bf16[96,576]{1,0:T(8,128)(2,1)S(1)}, bf16[96,576]{1,0:T(8,128)(2,1)S(1)}, u32[]{:S(2)}, u32[]{:S(2)}) %collective-permute-start.54) | collective-permute-done | bytes 110624 | tf_op jit(solution)/shard_map/ppermute | solution.py:1006
  (405 shorter events, 109.7 us)
Async XLA Ops:
  36.6 27.2 %collective-permute-start.8 = (bf16[2,96,1536]{2,1,0:T(8,128)(2,1)S(1)}, bf16[2,96,1536]{2,1,0:T(8,128)(2,1)}, u32[]{:S(2)}, u32[]{:S(2)}) collective-permute-start(bf16[2,96,1536]{2,1,0:T(8,128)(2,1)S(1)} %pad_maximum_fusion.5), channel_id=1, source_target_pairs={{0,2},{1,3},{2,0},{3,1},{4,6},{5,7},{6,4},{7,5},{8,10},{9,11},{10,... | collective-permute-start | bytes 1769480 | tf_op jit(solution)/shard_map/ppermute | solution.py:645
  39.9 27.0 %collective-permute-start.5 = (bf16[4,192,384]{2,1,0:T(8,128)(2,1)S(1)}, bf16[4,192,384]{2,1,0:T(8,128)(2,1)S(1)}, u32[]{:S(2)}, u32[]{:S(2)}) collective-permute-start(bf16[4,192,384]{2,1,0:T(8,128)(2,1)S(1)} %maximum_select_fusion.refs_2_), channel_id=1, source_target_pairs={{0,8},{4,12},{8,0},{12,4},{16,24},{20,28},{24,16},{28,20},{1,9},{5... | collective-permute-start | bytes 1769480 | tf_op jit(solution)/shard_map/ppermute | solution.py:648
  41.4 25.5 %collective-permute-start.6 = (bf16[4,192,384]{2,1,0:T(8,128)(2,1)S(1)}, bf16[4,192,384]{2,1,0:T(8,128)(2,1)S(1)}, u32[]{:S(2)}, u32[]{:S(2)}) collective-permute-start(bf16[4,192,384]{2,1,0:T(8,128)(2,1)S(1)} %maximum_select_fusion.refs_2_), channel_id=1, source_target_pairs={{0,16},{4,20},{8,24},{12,28},{16,0},{20,4},{24,8},{28,12},{1,17},{... | collective-permute-start | bytes 1769480 | tf_op jit(solution)/shard_map/ppermute | solution.py:648
  43.0 24.0 %collective-permute-start.7 = (bf16[4,192,384]{2,1,0:T(8,128)(2,1)S(1)}, bf16[4,192,384]{2,1,0:T(8,128)(2,1)S(1)}, u32[]{:S(2)}, u32[]{:S(2)}) collective-permute-start(bf16[4,192,384]{2,1,0:T(8,128)(2,1)S(1)} %maximum_select_fusion.refs_2_), channel_id=1, source_target_pairs={{0,24},{4,28},{8,16},{12,20},{16,8},{20,12},{24,0},{28,4},{1,25},{... | collective-permute-start | bytes 1769480 | tf_op jit(solution)/shard_map/ppermute | solution.py:648
  65.1 21.8 %collective-permute-start.10 = (bf16[512,768]{1,0:T(8,128)(2,1)}, bf16[512,768]{1,0:T(8,128)(2,1)S(1)}, u32[]{:S(2)}, u32[]{:S(2)}) collective-permute-start(bf16[512,768]{1,0:T(8,128)(2,1)} %get-tuple-element.352), channel_id=1, source_target_pairs={{0,1},{1,0},{2,5},{3,4},{4,3},{5,2},{6,7},{7,6},{8,9},{9,8},{10,13... | collective-permute-start | bytes 2359304 | tf_op jit(solution)/shard_map/ppermute | solution.py:663
  65.1 21.7 %collective-permute-start.9 = (bf16[512,768]{1,0:T(8,128)(2,1)}, bf16[512,768]{1,0:T(8,128)(2,1)S(1)}, u32[]{:S(2)}, u32[]{:S(2)}) collective-permute-start(bf16[512,768]{1,0:T(8,128)(2,1)} %get-tuple-element.351), channel_id=1, source_target_pairs={{0,0},{1,1},{2,4},{3,5},{4,2},{5,3},{6,6},{7,7},{8,8},{9,9},{10,12... | collective-permute-start | bytes 2359304 | tf_op jit(solution)/shard_map/ppermute | solution.py:663
  67.1 20.9 %collective-permute-start.13 = (bf16[4,192,384]{2,1,0:T(8,128)(2,1)S(1)}, bf16[4,192,384]{2,1,0:T(8,128)(2,1)}, u32[]{:S(2)}, u32[]{:S(2)}) collective-permute-start(bf16[4,192,384]{2,1,0:T(8,128)(2,1)S(1)} %pad_maximum_fusion.6.refs_0_), channel_id=1, source_target_pairs={{0,4},{4,0},{8,12},{12,8},{16,20},{20,16},{24,28},{28,24},{1,5},{5... | collective-permute-start | bytes 1769480 | tf_op jit(solution)/shard_map/ppermute | solution.py:642
  70.1 18.0 %collective-permute-start.11 = (bf16[2,96,1536]{2,1,0:T(8,128)(2,1)S(1)}, bf16[2,96,1536]{2,1,0:T(8,128)(2,1)S(1)}, u32[]{:S(2)}, u32[]{:S(2)}) collective-permute-start(bf16[2,96,1536]{2,1,0:T(8,128)(2,1)S(1)} %pad_maximum_fusion.5), channel_id=1, source_target_pairs={{0,8},{4,12},{8,0},{12,4},{16,24},{20,28},{24,16},{28,20},{1,9},{5... | collective-permute-start | bytes 1769480 | tf_op jit(solution)/shard_map/ppermute | solution.py:648
  71.6 16.5 %collective-permute-start.12 = (bf16[2,96,1536]{2,1,0:T(8,128)(2,1)}, bf16[2,96,1536]{2,1,0:T(8,128)(2,1)}, u32[]{:S(2)}, u32[]{:S(2)}) collective-permute-start(bf16[2,96,1536]{2,1,0:T(8,128)(2,1)} %collective-permute-done.8), channel_id=1, source_target_pairs={{0,16},{4,20},{8,24},{12,28},{16,0},{20,4},{24,8},{28,12},{1,17},{... | collective-permute-start | bytes 1769480 | tf_op jit(solution)/shard_map/ppermute | solution.py:648
  88.1 20.8 %collective-permute-start.14 = (bf16[1024,768]{1,0:T(8,128)(2,1)}, bf16[1024,768]{1,0:T(8,128)(2,1)}, u32[]{:S(2)}, u32[]{:S(2)}) collective-permute-start(bf16[1024,768]{1,0:T(8,128)(2,1)} %pad_maximum_fusion.refs_0_.refs_10_.xa_ref), channel_id=1, source_target_pairs={{0,4},{4,0},{8,12},{12,8},{16,20},{20,16},{24,28},{28,24},{1,5},{5... | collective-permute-start | bytes 4718600 | tf_op jit(solution)/shard_map/ppermute | solution.py:642
  105.2 34.4 %collective-permute-start.19 = (bf16[2,2,96,1536]{3,2,1,0:T(8,128)(2,1)S(1)}, bf16[2,2,96,1536]{3,2,1,0:T(8,128)(2,1)}, u32[]{:S(2)}, u32[]{:S(2)}) collective-permute-start(bf16[2,2,96,1536]{3,2,1,0:T(8,128)(2,1)S(1)} %pad_maximum_fusion.4.refs_3_), channel_id=1, source_target_pairs={{0,8},{4,12},{8,0},{12,4},{16,24},{20,28},{24,16},{28,20},{1,9},{5... | collective-permute-start | bytes 3538952 | tf_op jit(solution)/shard_map/ppermute | solution.py:648
  106.8 32.9 %collective-permute-start.18 = (bf16[2,2,96,1536]{3,2,1,0:T(8,128)(2,1)}, bf16[2,2,96,1536]{3,2,1,0:T(8,128)(2,1)}, u32[]{:S(2)}, u32[]{:S(2)}) collective-permute-start(bf16[2,2,96,1536]{3,2,1,0:T(8,128)(2,1)} %pad_maximum_fusion.3.refs_2_), channel_id=1, source_target_pairs={{0,16},{4,20},{8,24},{12,28},{16,0},{20,4},{24,8},{28,12},{1,17},{... | collective-permute-start | bytes 3538952 | tf_op jit(solution)/shard_map/ppermute | solution.py:648
  109.1 30.6 %collective-permute-start.20 = (bf16[512,768]{1,0:T(8,128)(2,1)S(1)}, bf16[512,768]{1,0:T(8,128)(2,1)S(1)}, u32[]{:S(2)}, u32[]{:S(2)}) collective-permute-start(bf16[512,768]{1,0:T(8,128)(2,1)S(1)} %get-tuple-element.350), channel_id=1, source_target_pairs={{0,0},{1,1},{2,4},{3,5},{4,2},{5,3},{6,6},{7,7},{8,8},{9,9},{10,12... | collective-permute-start | bytes 2359304 | tf_op jit(solution)/shard_map/ppermute | solution.py:663
  109.8 29.9 %collective-permute-start.21 = (bf16[512,768]{1,0:T(8,128)(2,1)S(1)}, bf16[512,768]{1,0:T(8,128)(2,1)S(1)}, u32[]{:S(2)}, u32[]{:S(2)}) collective-permute-start(bf16[512,768]{1,0:T(8,128)(2,1)S(1)} %get-tuple-element.349), channel_id=1, source_target_pairs={{0,1},{1,0},{2,5},{3,4},{4,3},{5,2},{6,7},{7,6},{8,9},{9,8},{10,13... | collective-permute-start | bytes 2359304 | tf_op jit(solution)/shard_map/ppermute | solution.py:663
  218.3 16.6 %collective-permute-start.26 = (bf16[4,4,96,768]{3,2,1,0:T(8,128)(2,1)}, bf16[4,4,96,768]{3,2,1,0:T(8,128)(2,1)S(1)}, u32[]{:S(2)}, u32[]{:S(2)}) collective-permute-start(bf16[4,4,96,768]{3,2,1,0:T(8,128)(2,1)} %get-tuple-element.200), channel_id=1, source_target_pairs={{0,4},{4,0},{8,12},{12,8},{16,20},{20,16},{24,28},{28,24},{1,5},{5... | collective-permute-start | bytes 7077896 | tf_op jit(solution)/shard_map/ppermute | solution.py:642
  232.6 19.8 %collective-permute-start.29 = (bf16[5,4,96,768]{3,2,1,0:T(8,128)(2,1)}, bf16[5,4,96,768]{3,2,1,0:T(8,128)(2,1)S(1)}, u32[]{:S(2)}, u32[]{:S(2)}) collective-permute-start(bf16[5,4,96,768]{3,2,1,0:T(8,128)(2,1)} %get-tuple-element.218), channel_id=1, source_target_pairs={{0,4},{4,0},{8,12},{12,8},{16,20},{20,16},{24,28},{28,24},{1,5},{5... | collective-permute-start | bytes 8847368 | tf_op jit(solution)/shard_map/ppermute | solution.py:642
  233.1 19.3 %collective-permute-start.30 = (bf16[512,768]{1,0:T(8,128)(2,1)}, bf16[512,768]{1,0:T(8,128)(2,1)S(1)}, u32[]{:S(2)}, u32[]{:S(2)}) collective-permute-start(bf16[512,768]{1,0:T(8,128)(2,1)} %get-tuple-element.219), channel_id=1, source_target_pairs={{0,0},{1,1},{4,2},{5,3},{2,4},{3,5},{6,6},{7,7},{8,8},{9,9},{12,10... | collective-permute-start | bytes 2359304 | tf_op jit(solution)/shard_map/ppermute | solution.py:799
  261.0 23.4 %collective-permute-start.33 = (bf16[3,2,96,768]{3,2,0,1:T(8,128)(2,1)}, bf16[3,2,96,768]{3,2,0,1:T(8,128)(2,1)S(1)}, u32[]{:S(2)}, u32[]{:S(2)}) collective-permute-start(bf16[3,2,96,768]{3,2,0,1:T(8,128)(2,1)} %add_convert_fusion), channel_id=1, source_target_pairs={{0,8},{4,12},{8,0},{12,4},{16,24},{20,28},{24,16},{28,20},{1,9},{5... | collective-permute-start | bytes 2654216 | tf_op jit(solution)/shard_map/ppermute | solution.py:648
  261.7 22.8 %collective-permute-start.34 = (bf16[2,2,96,768]{3,2,0,1:T(8,128)(2,1)}, bf16[2,2,96,768]{3,2,0,1:T(8,128)(2,1)S(1)}, u32[]{:S(2)}, u32[]{:S(2)}) collective-permute-start(bf16[2,2,96,768]{3,2,0,1:T(8,128)(2,1)} %add_convert_fusion.1), channel_id=1, source_target_pairs={{0,16},{4,20},{8,24},{12,28},{16,0},{20,4},{24,8},{28,12},{1,17},{... | collective-permute-start | bytes 1769480 | tf_op jit(solution)/shard_map/ppermute | solution.py:648
  262.9 16.4 %collective-permute-start.31 = (bf16[2,96,768]{2,1,0:T(8,128)(2,1)S(1)}, bf16[2,96,768]{2,1,0:T(8,128)(2,1)S(1)}, u32[]{:S(2)}, u32[]{:S(2)}) collective-permute-start(bf16[2,96,768]{2,1,0:T(8,128)(2,1)S(1)} %get-tuple-element.230), channel_id=1, source_target_pairs={{0,16},{4,20},{8,24},{12,28},{16,0},{20,4},{24,8},{28,12},{1,17},{... | collective-permute-start | bytes 884744 | tf_op jit(solution)/shard_map/ppermute | solution.py:648
  263.7 20.7 %collective-permute-start.32 = (bf16[2,96,768]{2,1,0:T(8,128)(2,1)}, bf16[2,96,768]{2,1,0:T(8,128)(2,1)}, u32[]{:S(2)}, u32[]{:S(2)}) collective-permute-start(bf16[2,96,768]{2,1,0:T(8,128)(2,1)} %fusion.18), channel_id=1, source_target_pairs={{0,8},{4,12},{8,0},{12,4},{16,24},{20,28},{24,16},{28,20},{1,9},{5... | collective-permute-start | bytes 884744 | tf_op jit(solution)/shard_map/ppermute | solution.py:648
  291.0 27.1 %collective-permute-start.35 = (bf16[3,96,768]{2,1,0:T(8,128)(2,1)S(1)}, bf16[3,96,768]{2,1,0:T(8,128)(2,1)S(1)}, u32[]{:S(2)}, u32[]{:S(2)}) collective-permute-start(bf16[3,96,768]{2,1,0:T(8,128)(2,1)S(1)} %get-tuple-element.247), channel_id=1, source_target_pairs={{0,16},{4,20},{8,24},{12,28},{16,0},{20,4},{24,8},{28,12},{1,17},{... | collective-permute-start | bytes 1327112 | tf_op jit(solution)/shard_map/ppermute | solution.py:648
  291.3 26.9 %collective-permute-start.36 = (bf16[2,96,768]{2,1,0:T(8,128)(2,1)}, bf16[2,96,768]{2,1,0:T(8,128)(2,1)S(1)}, u32[]{:S(2)}, u32[]{:S(2)}) collective-permute-start(bf16[2,96,768]{2,1,0:T(8,128)(2,1)} %fusion.19), channel_id=1, source_target_pairs={{0,8},{4,12},{8,0},{12,4},{16,24},{20,28},{24,16},{28,20},{1,9},{5... | collective-permute-start | bytes 884744 | tf_op jit(solution)/shard_map/ppermute | solution.py:648
  292.4 25.8 %collective-permute-start.37 = (bf16[2,96,768]{2,1,0:T(8,128)(2,1)S(1)}, bf16[2,96,768]{2,1,0:T(8,128)(2,1)S(1)}, u32[]{:S(2)}, u32[]{:S(2)}) collective-permute-start(bf16[2,96,768]{2,1,0:T(8,128)(2,1)S(1)} %add_convert_fusion.5), channel_id=1, source_target_pairs={{0,2},{1,3},{2,0},{3,1},{4,6},{5,7},{6,4},{7,5},{8,10},{9,11},{10,... | collective-permute-start | bytes 884744 | tf_op jit(solution)/shard_map/ppermute | solution.py:645
  303.5 35.4 %collective-permute-start.41 = (bf16[512,768]{1,0:T(8,128)(2,1)}, bf16[512,768]{1,0:T(8,128)(2,1)}, u32[]{:S(2)}, u32[]{:S(2)}) collective-permute-start(bf16[512,768]{1,0:T(8,128)(2,1)} %get-tuple-element.266), channel_id=1, source_target_pairs={{1,0},{0,1},{5,2},{4,3},{3,4},{2,5},{7,6},{6,7},{9,8},{8,9},{13,10... | collective-permute-start | bytes 2359304 | tf_op jit(solution)/shard_map/ppermute | solution.py:896
  322.2 29.0 %collective-permute-start.39 = (bf16[3,96,768]{2,1,0:T(8,128)(2,1)S(1)}, bf16[3,96,768]{2,1,0:T(8,128)(2,1)S(1)}, u32[]{:S(2)}, u32[]{:S(2)}) collective-permute-start(bf16[3,96,768]{2,1,0:T(8,128)(2,1)S(1)} %pad_maximum_fusion.7), channel_id=1, source_target_pairs={{0,2},{1,3},{2,0},{3,1},{4,6},{5,7},{6,4},{7,5},{8,10},{9,11},{10,... | collective-permute-start | bytes 1327112 | tf_op jit(solution)/shard_map/ppermute | solution.py:645
  322.2 16.8 %collective-permute-start.38 = (bf16[96,768]{1,0:T(8,128)(2,1)S(1)}, bf16[96,768]{1,0:T(8,128)(2,1)S(1)}, u32[]{:S(2)}, u32[]{:S(2)}) collective-permute-start(bf16[96,768]{1,0:T(8,128)(2,1)S(1)} %get-tuple-element.263), channel_id=1, source_target_pairs={{0,1},{1,0},{2,3},{3,2},{4,5},{5,4},{6,7},{7,6},{8,9},{9,8},{10,11... | collective-permute-start | bytes 442376 | tf_op jit(solution)/shard_map/ppermute | solution.py:645
  352.8 19.2 %collective-permute-start.42 = (bf16[1024,768]{1,0:T(8,128)(2,1)S(1)}, bf16[1024,768]{1,0:T(8,128)(2,1)S(1)}, u32[]{:S(2)}, u32[]{:S(2)}) collective-permute-start(bf16[1024,768]{1,0:T(8,128)(2,1)S(1)} %copy-done.9), channel_id=1, source_target_pairs={{0,4},{4,0},{8,12},{12,8},{16,20},{20,16},{24,28},{28,24},{1,5},{5... | collective-permute-start | bytes 4718600 | tf_op jit(solution)/shard_map/ppermute | solution.py:642
  393.6 19.1 %collective-permute-start.49 = (bf16[512,768]{1,0:T(8,128)(2,1)}, bf16[512,768]{1,0:T(8,128)(2,1)S(1)}, u32[]{:S(2)}, u32[]{:S(2)}) collective-permute-start(bf16[512,768]{1,0:T(8,128)(2,1)} %get-tuple-element.289), channel_id=1, source_target_pairs={{1,0},{0,1},{5,2},{4,3},{3,4},{2,5},{7,6},{6,7},{9,8},{8,9},{13,10... | collective-permute-start | bytes 2359304 | tf_op jit(solution)/shard_map/ppermute | solution.py:974
  415.7 23.2 %collective-permute-start.52 = (bf16[96,576]{1,0:T(8,128)(2,1)S(1)}, bf16[96,576]{1,0:T(8,128)(2,1)S(1)}, u32[]{:S(2)}, u32[]{:S(2)}) collective-permute-start(bf16[96,576]{1,0:T(8,128)(2,1)S(1)} %broadcast_select_fusion.17), channel_id=1, source_target_pairs={{0,0},{1,1},{2,4},{3,5},{4,2},{5,3},{6,6},{7,7},{8,8},{9,9},{10,12... | collective-permute-start | bytes 331784 | tf_op jit(solution)/shard_map/ppermute | solution.py:1006
  416.4 22.6 %collective-permute-start.53 = (bf16[96,576]{1,0:T(8,128)(2,1)S(1)}, bf16[96,576]{1,0:T(8,128)(2,1)S(1)}, u32[]{:S(2)}, u32[]{:S(2)}) collective-permute-start(bf16[96,576]{1,0:T(8,128)(2,1)S(1)} %broadcast_select_fusion.16), channel_id=1, source_target_pairs={{0,1},{1,0},{2,5},{3,4},{4,3},{5,2},{6,7},{7,6},{8,9},{9,8},{10,13... | collective-permute-start | bytes 331784 | tf_op jit(solution)/shard_map/ppermute | solution.py:1006
  418.8 29.0 %collective-permute-start.54 = (bf16[96,576]{1,0:T(8,128)(2,1)S(1)}, bf16[96,576]{1,0:T(8,128)(2,1)S(1)}, u32[]{:S(2)}, u32[]{:S(2)}) collective-permute-start(bf16[96,576]{1,0:T(8,128)(2,1)S(1)} %broadcast_select_fusion.11), channel_id=1, source_target_pairs={{0,4},{1,5},{2,0},{3,1},{4,6},{5,7},{6,2},{7,3},{8,12},{9,13},{10,... | collective-permute-start | bytes 331784 | tf_op jit(solution)/shard_map/ppermute | solution.py:1006
  (94 other events, 1085.6 us)
